TPU v7x, 512 devices: a whole 4x8x8 slice. The times are simulated.
512 devices in a mesh: dop: 32 (over z, x), rng: 16 (over y, core).
Axes of the slice: x: 4, y: 8, z: 8, core: 2. Of those that a mesh axis runs over, the one named last changes fastest.
Arguments:
- raw_samples: bfloat16 [256, 384, 2, 4096], P('dop', 'rng'), may hold values from -16 to 16
- filter_taps: float32 [8, 512], replicated, may hold values from -2 to 2
- range_code: float32 [2, 7], replicated, may hold values from -1.6 to 1.6
- train_mask: int32 [64, 384], P('dop', 'rng'), may hold values 0 or 1
- steer_index: int32 [64, 4], P('dop'), may hold values from 0 to 255
Outputs:
- beam_out: float32 [2, 64, 4, 384], P(None, 'dop', None, 'rng')
All inputs are finite; a program needn't handle non-finite values. No bound on the sum of `train_mask` on one device may be relied on, other than what follows from the above.
Results may differ from a plain program's by a relative error of at most 0.012.
The roundings to bfloat16 on the way count: a program that leaves them out, or rounds other values in their place, can miss the bound.
Values may be sent and summed in bfloat16 or wider, within the bound.
No kernel may reach another device: no remote copies, remote signals or barrier semaphores. Data moves between devices by JAX's collectives and lax.ppermute only.
A program may use at most 64 MiB of HBM per device.

v0:
```python
import math

import jax
import jax.numpy as jnp
from jax import lax
from jax.sharding import PartitionSpec as P

ELEMENTS = 256
CHANNELS = 512
TAPS = 8
CODE_REACH = 3


loading_level = 0.25


def padded_2(x, sides, width):
    for axis, dim in sides:
        count, length = (lax.axis_size(axis), x.shape[dim])
        up = [(i, (i + 1) % count) for i in range(count - 1)]
        down = [(j, i) for i, j in up]
        last = lax.slice_in_dim(x, length - width, length, axis=dim)
        leading = lax.slice_in_dim(x, 0, width, axis=dim)
        before = lax.ppermute(last, axis, up)
        after = lax.ppermute(leading, axis, down)
        x = jnp.concatenate([before, x, after], axis=dim)
    return x


def dft_table(bin_total):
    mode_index = jnp.arange(CHANNELS, dtype=jnp.int32)
    bin_index = jnp.arange(bin_total, dtype=jnp.int32)
    turn_count = jnp.mod(mode_index[:, None] * bin_index[None, :], CHANNELS).astype(jnp.float32)
    phases = turn_count * (2.0 * math.pi / CHANNELS)
    cosine = jnp.cos(phases) / math.sqrt(CHANNELS)
    sine_part = jnp.sin(phases) / math.sqrt(CHANNELS)
    top_half = jnp.concatenate([cosine, -sine_part], axis=1)
    low_half = jnp.concatenate([sine_part, cosine], axis=1)
    return jnp.concatenate([top_half, low_half], axis=0).astype(jnp.bfloat16)


def compress(padded, range_code):
    gate_count = padded.shape[1] - 2 * CODE_REACH
    shape_out = (padded.shape[0], gate_count, padded.shape[3])
    real_sum = jnp.zeros(shape_out, jnp.float32)
    imag_sum = jnp.zeros(shape_out, jnp.float32)
    for offset in range(2 * CODE_REACH + 1):
        window = lax.slice_in_dim(padded, offset, offset + gate_count, axis=1).astype(jnp.float32)
        real_sum = (
            real_sum
            + range_code[0, offset] * window[:, :, 0]
            - range_code[1, offset] * window[:, :, 1]
        )
        imag_sum = (
            imag_sum
            + range_code[0, offset] * window[:, :, 1]
            + range_code[1, offset] * window[:, :, 0]
        )
    return jnp.stack([real_sum, imag_sum], axis=2).astype(jnp.bfloat16)


def half_terms(masked):
    real_rows = masked[:, :, 0]
    imag_rows = masked[:, :, 1]
    left_rows = jnp.concatenate([real_rows, imag_rows], axis=1)
    right_rows = jnp.concatenate([imag_rows, -real_rows], axis=1)
    symmetric = jnp.einsum("bri,brj->bij", left_rows, left_rows, preferred_element_type=jnp.float32)
    skewed = jnp.einsum("bri,brj->bij", right_rows, left_rows, preferred_element_type=jnp.float32)
    return (symmetric, skewed)


def steering_table(steer_rows):
    element = jnp.arange(ELEMENTS, dtype=jnp.int32)
    turn_count = jnp.mod(
        element[None, :, None] * (2 * steer_rows[:, None, :] - ELEMENTS), 2 * ELEMENTS
    ).astype(jnp.float32)
    phases = turn_count * (math.pi / ELEMENTS)
    return jnp.concatenate([jnp.cos(phases), jnp.sin(phases)], axis=1)


def solve_all(factor, steering):
    return jax.vmap(
        lambda lower_part, target: jax.scipy.linalg.cho_solve((lower_part, True), target)
    )(factor, steering)


def beam_output(compressed, weights, steering):
    response = jnp.sum(steering * weights, axis=1)
    signal = compressed.astype(jnp.float32)
    weight_real = weights[:, :ELEMENTS]
    weight_imag = weights[:, ELEMENTS:]
    highest = lax.Precision.HIGHEST
    out_real = jnp.einsum(
        "bik,bgi->bkg", weight_real, signal[:, :, 0], precision=highest
    ) + jnp.einsum("bik,bgi->bkg", weight_imag, signal[:, :, 1], precision=highest)
    out_imag = jnp.einsum(
        "bik,bgi->bkg", weight_real, signal[:, :, 1], precision=highest
    ) - jnp.einsum("bik,bgi->bkg", weight_imag, signal[:, :, 0], precision=highest)
    return jnp.stack([out_real, out_imag], axis=0) / jnp.sqrt(response)[None, :, :, None]


def shards(raw_samples, filter_taps, range_code, train_mask, steer_index):
    elem_dev = raw_samples.shape[0]
    gate_dev = raw_samples.shape[1]
    bin_dev = train_mask.shape[0]
    bin_total = bin_dev * lax.axis_size("dop")
    gates_total = gate_dev * lax.axis_size("rng")
    table = dft_table(bin_total)
    folded = raw_samples.astype(jnp.float32).reshape(elem_dev, gate_dev, 2, TAPS, CHANNELS)
    filtered = jnp.sum(folded * filter_taps, axis=3).astype(jnp.bfloat16)
    spectra = jnp.dot(
        filtered.reshape(elem_dev * gate_dev, 2 * CHANNELS),
        table,
        preferred_element_type=jnp.float32,
    )
    spectra = jnp.transpose(
        spectra.astype(jnp.bfloat16).reshape(elem_dev, gate_dev, 2, bin_total), (3, 1, 2, 0)
    )
    turned = lax.all_to_all(spectra, "dop", split_axis=0, concat_axis=3, tiled=True)
    padded = padded_2(turned, (("rng", 1),), CODE_REACH)
    compressed = compress(padded, range_code)
    masked = compressed * train_mask.astype(jnp.bfloat16)[:, :, None, None]
    dof_count = 2 * ELEMENTS
    identity = jnp.eye(dof_count, dtype=jnp.float32)
    steering = steering_table(steer_index)
    symmetric, skewed = half_terms(masked)
    symmetric, skewed = lax.psum((symmetric, skewed), "rng")
    top_block = jnp.concatenate([symmetric, -skewed], axis=2)
    low_block = jnp.concatenate([skewed, symmetric], axis=2)
    summed = jnp.concatenate([top_block, low_block], axis=1)
    factor = jnp.linalg.cholesky(summed / gates_total + loading_level * identity)
    weights = solve_all(factor, steering)
    return beam_output(compressed, weights, steering)


def solution(mesh):
    return jax.shard_map(
        shards,
        mesh=mesh,
        in_specs=(P("dop", "rng", None, None), P(), P(), P("dop", "rng"), P("dop", None)),
        out_specs=P(None, "dop", None, "rng"),
        check_vma=False,
    )
```

profile of v0, /device:TPU:1, one launch (start us, length us, event | category | flops | bytes accessed | tf_op | source)
XLA Modules:
  0.0 470.4 jit_solution(3311249584527519033)
XLA Ops:
  7.6 6.4 %reshape.119 = f32[8,24,2,8,512]{4,3,2,1,0:T(8,128)} reshape(bf16[8,24,2,4096]{3,2,1,0:T(2,128)(2,1)} %param.5) | data formatting | bytes 9437184 | tf_op jit(solution)/shard_map/reshape | solution.py:109
  14.0 5.5 %multiply_reduce_fusion = bf16[8,24,2,512]{3,2,1,0:T(2,128)(2,1)S(1)} fusion(f32[8,24,2,8,512]{4,3,2,1,0:T(8,128)} %reshape.119, f32[8,512]{1,0:T(8,128)S(1)} %copy-done.2), kind=kLoop, calls=%fused_computation.2 | loop fusion | flops 2949120 | bytes 6701056 | tf_op jit(solution)/shard_map/reduce_sum | solution.py:110
  21.2 13.7 %all-to-all-start = ((bf16[32,2,384]{2,1,0:T(2,128)(2,1)}), bf16[32,2,384]{2,1,0:T(2,128)(2,1)S(1)}, u32[]{:S(2)}, u32[]{:S(2)}) async-start(bf16[32,2,384]{2,1,0:T(2,128)(2,1)} %reshape.120), calls=%async_computation | async-start | bytes 98304 | tf_op jit(solution)/shard_map/all_to_all | solution.py:119
  35.9 7.8 %all-to-all-done = bf16[32,2,384]{2,1,0:T(2,128)(2,1)S(1)} async-done(((bf16[32,2,384]{2,1,0:T(2,128)(2,1)}), bf16[32,2,384]{2,1,0:T(2,128)(2,1)S(1)}, u32[]{:S(2)}, u32[]{:S(2)}) %all-to-all-start) | async-done | bytes 49184 | tf_op jit(solution)/shard_map/all_to_all | solution.py:119
  44.2 5.1 %collective-permute-start = (bf16[2,3,2,256]{3,1,0,2:T(4,128)(2,1)S(1)}, bf16[2,3,2,256]{3,1,0,2:T(4,128)(2,1)S(1)}, u32[]{:S(2)}, u32[]{:S(2)}) collective-permute-start(bf16[2,3,2,256]{3,1,0,2:T(4,128)(2,1)S(1)} %get-tuple-element.46), channel_id=1, source_target_pairs={{0,1},{1,2},{2,3},{3,4},{4,5},{5,6},{6,7},{7,8},{8,9},{9,10},{10,1... | collective-permute-start | bytes 18440 | tf_op jit(solution)/shard_map/ppermute | solution.py:24
  51.3 3.0 collective-permute-done.1
  54.4 8.8 %subtract_convert_fusion = bf16[2,24,1,256]{3,1,0,2:T(8,128)(2,1)S(1)} fusion(f32[2,24,2,256]{3,1,0,2:T(8,128)S(1)} %get-tuple-element.43, f32[2,24,2,256]{3,1,0,2:T(8,128)S(1)} %get-tuple-element.42, f32[2,24,2,256]{3,1,0,2:T(8,128)S(1)} %get-tuple-element.44, f32[2,24,2,256]{3,1,0,2:T(8,128)S(1)} %get-tuple-element.45, ...), kind=kLoop, calls=%fused_computation.113 | loop fusion | flops 344064 | bytes 712760 | tf_op jit(solution)/shard_map/slice | solution.py:94
  63.2 8.7 %add_convert_fusion = bf16[2,24,1,256]{3,1,0,2:T(8,128)(2,1)S(1)} fusion(f32[2,24,2,256]{3,1,0,2:T(8,128)S(1)} %get-tuple-element.43, f32[2,24,2,256]{3,1,0,2:T(8,128)S(1)} %get-tuple-element.42, f32[2,24,2,256]{3,1,0,2:T(8,128)S(1)} %get-tuple-element.44, f32[2,24,2,256]{3,1,0,2:T(8,128)S(1)} %get-tuple-element.45, ...), kind=kLoop, calls=%fused_computation.112 | loop fusion | flops 344064 | bytes 712760 | tf_op jit(solution)/shard_map/slice | solution.py:95
  74.4 112.1 %all-reduce.4.cloned.1.call-done = (f32[2,256,256]{1,2,0:T(8,128)}, f32[2,256,256]{1,2,0:T(8,128)}) async-done(((f32[2,256,256]{1,2,0:T(8,128)}, f32[2,256,256]{1,2,0:T(8,128)}), (f32[2,256,256]{1,2,0:T(8,128)}, f32[2,256,256]{1,2,0:T(8,128)})) %all-reduce.4.cloned.1.call-update) | async-done | bytes 1048592 | tf_op jit(solution)/shard_map/psum | solution.py:127
  189.4 2.1 copy.82
  191.4 2.1 fusion.1
  194.9 23.5 %custom-call.38 = f32[2,128,128]{2,1,0:T(8,128)S(1)} custom-call(f32[2,128,128]{2,1,0:T(8,128)S(1)} %cholesky.274), custom_call_target="Cholesky" | custom-call | tf_op jit(solution)/shard_map/jit(cholesky)/cholesky | solution.py:131
  218.6 19.7 %custom-call.39 = f32[2,1,128,128]{2,3,1,0:T(8,128)S(1)} custom-call(f32[2,1,128,128]{3,2,1,0:T(8,128)S(1)} %select_bitcast_fusion.2), custom_call_target="InvertDiagBlocksLowerTriangular" | custom-call | tf_op jit(solution)/shard_map/jit(cholesky)/cholesky | solution.py:131
  241.3 23.5 %custom-call.40 = f32[2,128,128]{2,1,0:T(8,128)S(1)} custom-call(f32[2,128,128]{2,1,0:T(8,128)S(1)} %cholesky.278), custom_call_target="Cholesky" | custom-call | tf_op jit(solution)/shard_map/jit(cholesky)/cholesky | solution.py:131
  264.8 19.9 %custom-call.41 = f32[2,1,128,128]{2,3,1,0:T(8,128)S(1)} custom-call(f32[2,1,128,128]{3,2,1,0:T(8,128)S(1)} %get-tuple-element.32), custom_call_target="InvertDiagBlocksLowerTriangular" | custom-call | tf_op jit(solution)/shard_map/jit(cholesky)/cholesky | solution.py:131
  286.7 23.5 %custom-call.42 = f32[2,128,128]{2,1,0:T(8,128)S(1)} custom-call(f32[2,128,128]{2,1,0:T(8,128)S(1)} %cholesky.283), custom_call_target="Cholesky" | custom-call | tf_op jit(solution)/shard_map/jit(cholesky)/cholesky | solution.py:131
  310.2 19.7 %custom-call.43 = f32[2,1,128,128]{2,3,1,0:T(8,128)S(1)} custom-call(f32[2,1,128,128]{3,2,1,0:T(8,128)S(1)} %get-tuple-element.30), custom_call_target="InvertDiagBlocksLowerTriangular" | custom-call | tf_op jit(solution)/shard_map/jit(cholesky)/cholesky | solution.py:131
  331.7 23.7 %custom-call.44 = f32[2,128,128]{2,1,0:T(8,128)S(1)} custom-call(f32[2,128,128]{2,1,0:T(8,128)S(1)} %convolution_subtract_fusion.2), custom_call_target="Cholesky" | custom-call | tf_op jit(solution)/shard_map/jit(cholesky)/cholesky | solution.py:131
  357.7 14.6 %while.1 = (s32[]{:T(128)}, f32[2,512,512]{2,1,0:T(8,128)}, s32[4,2]{0,1:T(2,128)S(1)}, f32[4,2,128,128]{3,2,0,1:T(8,128)}, s32[]{:T(128)}) while((s32[]{:T(128)}, f32[2,512,512]{2,1,0:T(8,128)}, s32[4,2]{0,1:T(2,128)S(1)}, f32[4,2,128,128]{3,2,0,1:T(8,128)}, s32[]{:T(128)}) %tuple.51), condition=%wide.while_cond, body=%wide.while_body.sunk | while | flops 2 | bytes 263777 | solution.py:83
  358.4 3.0 bitcast_dynamic-update-slice_fusion.2
  362.0 3.0 bitcast_dynamic-update-slice_fusion.2
  365.7 3.0 bitcast_dynamic-update-slice_fusion.2
  369.3 3.0 bitcast_dynamic-update-slice_fusion.2
  372.3 79.4 %custom-call.45 = f32[2,4,128,128]{2,3,1,0:T(8,128)S(1)} custom-call(f32[2,4,128,128]{3,2,1,0:T(8,128)} %bitcast.119), custom_call_target="InvertDiagBlocksLowerTriangular" | custom-call | tf_op jit(solution)/shard_map/vmap(jit(_cho_solve))/triangular_solve | solution.py:83
  (94 shorter events, 36.1 us)
Async XLA Ops:
  7.6 6.4 %copy-start.2 = (f32[8,512]{1,0:T(8,128)S(1)}, f32[8,512]{1,0:T(8,128)}, u32[]{:S(2)}) copy-start(f32[8,512]{1,0:T(8,128)} %param.6) | copy-start | bytes 49156
  19.6 15.6 %copy-start.1 = (f32[2,7]{1,0:T(2,128)S(1)}, f32[2,7]{1,0:T(2,128)}, u32[]{:S(2)}) copy-start(f32[2,7]{1,0:T(2,128)} %param.7) | copy-start | bytes 172
  19.8 31.5 %copy-start.4 = (s32[2,24]{1,0:T(2,128)S(1)}, s32[2,24]{1,0:T(2,128)}, u32[]{:S(2)}) copy-start(s32[2,24]{1,0:T(2,128)} %param.8) | copy-start | bytes 580
  21.2 22.5 %all-to-all-start = ((bf16[32,2,384]{2,1,0:T(2,128)(2,1)}), bf16[32,2,384]{2,1,0:T(2,128)(2,1)S(1)}, u32[]{:S(2)}, u32[]{:S(2)}) async-start(bf16[32,2,384]{2,1,0:T(2,128)(2,1)} %reshape.120), calls=%async_computation | async-start | bytes 98304 | tf_op jit(solution)/shard_map/all_to_all | solution.py:119
  34.9 151.6 %all-reduce.4.cloned.1.call-start = ((), (), s32[]{:S(2)}) async-start(), calls=%async_computation.1 | async-start | bytes 2097152 | tf_op jit(solution)/shard_map/psum | solution.py:127
  44.2 7.1 %collective-permute-start = (bf16[2,3,2,256]{3,1,0,2:T(4,128)(2,1)S(1)}, bf16[2,3,2,256]{3,1,0,2:T(4,128)(2,1)S(1)}, u32[]{:S(2)}, u32[]{:S(2)}) collective-permute-start(bf16[2,3,2,256]{3,1,0,2:T(4,128)(2,1)S(1)} %get-tuple-element.46), channel_id=1, source_target_pairs={{0,1},{1,2},{2,3},{3,4},{4,5},{5,6},{6,7},{7,8},{8,9},{9,10},{10,1... | collective-permute-start | bytes 18440 | tf_op jit(solution)/shard_map/ppermute | solution.py:24
  49.4 5.0 %collective-permute-start.1 = (bf16[2,3,2,256]{3,1,0,2:T(4,128)(2,1)S(1)}, bf16[2,3,2,256]{3,1,0,2:T(4,128)(2,1)S(1)}, u32[]{:S(2)}, u32[]{:S(2)}) collective-permute-start(bf16[2,3,2,256]{3,1,0,2:T(4,128)(2,1)S(1)} %get-tuple-element.47), channel_id=1, source_target_pairs={{1,0},{2,1},{3,2},{4,3},{5,4},{6,5},{7,6},{8,7},{9,8},{10,9},{11,1... | collective-permute-start | bytes 18440 | tf_op jit(solution)/shard_map/ppermute | solution.py:25
  54.4 19.8 %copy-start.3 = (s32[2,4]{1,0:T(2,128)S(1)}, s32[2,4]{1,0:T(2,128)}, u32[]{:S(2)}) copy-start(s32[2,4]{1,0:T(2,128)} %param.9) | copy-start | bytes 100
  193.5 1.4 copy-start
Sparse Core Ops, SparseCore 0:
  74.3 112.1 all-reduce.3
where the time goes:
time: 477 us; the launch traced here: 470 us
  other arithmetic  265 us (56%)
  waiting for transfers between devices  123 us (26%)
  local copies, waits for them, and re-layouts  27.3 us (6%)
  starting transfers between devices  20.8 us (4%)
  matrix products  19.7 us (4%)
  between operations  14.3 us (3%)
    another operation x18, other arithmetic, shards(): jnp.linalg.cholesky(summed / gates_total + loading_level * identity)  154 us
    psum x1, waiting for transfers between devices, shards(): symmetric, skewed = lax.psum((symmetric, skewed), 'rng')  112 us
    another operation x4, other arithmetic, solve_all(): jax.scipy.linalg.cho_solve((lower_part, True), target)  81.3 us
    another operation x12, local copies, waits for them, and re-layouts  14.6 us
    all_to_all x1, starting transfers between devices, shards(): lax.all_to_all(spectra, 'dop', split_axis=0, concat_axis=3, tiled=True)  13.7 us
    another operation x14, matrix products, solve_all(): jax.scipy.linalg.cho_solve((lower_part, True), target)  9.99 us
  transfers between devices with their start and end apart: 4, of which 3 were waited for; matrix products, arithmetic and copies ran while one was open for 0% of the time, Pallas kernels for 0%

commit v1 on v0

v1 whole, which is shorter than its diff:
```python
import math

import jax
import jax.numpy as jnp
import numpy as np
from jax import lax
from jax.experimental import pallas as pl
from jax.experimental.pallas import tpu as pltpu
from jax.sharding import PartitionSpec as P

CHANNELS = 512
TAPS = 8
CODE_REACH = 3
LOADING = 0.25
BLOCK = 32
STEP = 4
LANES = 128
HEAD = 8
MASK_ROWS = 8

HIGHEST = lax.Precision.HIGHEST


def dft_columns(bin_total):
    mode = np.arange(CHANNELS, dtype=np.int64)[:, None]
    turn = (mode * np.arange(bin_total, dtype=np.int64)[None, :]) % CHANNELS
    phases = turn.astype(np.float32) * np.float32(2.0 * math.pi / CHANNELS)
    scale = np.float32(math.sqrt(CHANNELS))
    both = np.concatenate([np.cos(phases) / scale, np.sin(phases) / scale], axis=1)
    return jnp.asarray(both, jnp.bfloat16)


def mm(a, b, dims, precision=HIGHEST):
    return lax.dot_general(
        a, b, (dims, ((), ())), precision=precision, preferred_element_type=jnp.float32
    )


NN = ((1,), (0,))
TN = ((0,), (0,))
NT = ((1,), (1,))


def eliminate(work, turned):
    rows = lax.broadcasted_iota(jnp.int32, work.shape, 0)
    scale = jnp.zeros_like(work)
    for base in range(0, BLOCK, STEP):
        col_re = [jnp.broadcast_to(work[:, base + t : base + t + 1], work.shape) for t in range(STEP)]
        col_im = [
            jnp.broadcast_to(work[:, BLOCK + base + t : BLOCK + base + t + 1], work.shape)
            for t in range(STEP)
        ]
        for t in range(STEP):
            j = base + t
            pivot = jnp.broadcast_to(col_re[t][j : j + 1], (8, LANES))
            inverse = jnp.concatenate([1.0 / pivot] * (BLOCK // 8), axis=0)
            below = rows > j
            m_re = jnp.where(below, col_re[t] * inverse, 0.0)
            m_im = jnp.where(below, col_im[t] * inverse, 0.0)
            for u in range(t + 1, STEP):
                e_re = jnp.broadcast_to(col_re[u][j : j + 1], work.shape)
                e_im = jnp.broadcast_to(col_im[u][j : j + 1], work.shape)
                col_re[u], col_im[u] = (
                    col_re[u] - m_re * e_re + m_im * e_im,
                    col_im[u] - m_re * e_im - m_im * e_re,
                )
            row = jnp.broadcast_to(work[j : j + 1], work.shape)
            row_turned = jnp.broadcast_to(turned[j : j + 1], work.shape)
            work, turned = (
                work - m_re * row - m_im * row_turned,
                turned - m_re * row_turned + m_im * row,
            )
            scale = jnp.where(rows == j, inverse, scale)
    scale = jnp.sqrt(scale)
    return work * scale, turned * scale


def adapt_kernel(
    place_ref,
    code_ref,
    chunks_ref,
    rhs_re_ref,
    rhs_im_ref,
    own_ref,
    other_ref,
    sig_re,
    sig_im,
    x_re,
    x_im,
    train,
    mat_re,
    mat_im,
    emb_ref,
    wts_ref,
):
    chunk_count, _, _, elements = chunks_ref.shape
    gate_dev = (chunks_ref.shape[2] - MASK_ROWS) // 2
    gates = chunk_count * gate_dev
    width = elements + LANES
    zero = jnp.zeros((HEAD, elements), jnp.float32)
    for ref in (sig_re, sig_im):
        ref[0:HEAD] = zero
        ref[HEAD + gates : 2 * HEAD + gates] = zero
    for c in range(chunk_count):
        chunk = chunks_ref[c, 0].astype(jnp.float32)
        at = HEAD + c * gate_dev
        sig_re[at : at + gate_dev] = chunk[:gate_dev]
        sig_im[at : at + gate_dev] = chunk[gate_dev : 2 * gate_dev]

    diagonal = lax.broadcasted_iota(jnp.int32, (gate_dev, LANES), 0) == lax.broadcasted_iota(
        jnp.int32, (gate_dev, LANES), 1
    )
    for c in range(chunk_count):
        at = c * gate_dev
        real = jnp.zeros((gate_dev, elements), jnp.float32)
        imag = jnp.zeros((gate_dev, elements), jnp.float32)
        for t in range(2 * CODE_REACH + 1):
            start = HEAD + at + t - CODE_REACH
            w_re = sig_re[start : start + gate_dev]
            w_im = sig_im[start : start + gate_dev]
            c_re, c_im = code_ref[0, t], code_ref[1, t]
            real = real + c_re * w_re - c_im * w_im
            imag = imag + c_re * w_im + c_im * w_re
        real = real.astype(jnp.bfloat16).astype(jnp.float32)
        imag = imag.astype(jnp.bfloat16).astype(jnp.float32)
        x_re[at : at + gate_dev] = real
        x_im[at : at + gate_dev] = imag
        mask_row = chunks_ref[c, 0, 2 * gate_dev : 2 * gate_dev + 8, :LANES].astype(jnp.float32)[:1]
        mask = jnp.sum(jnp.where(diagonal, mask_row, 0.0), axis=1, keepdims=True)
        train[at : at + gate_dev, :elements] = (real * mask).astype(jnp.bfloat16)
        train[at : at + gate_dev, elements:] = (imag * mask).astype(jnp.bfloat16)

    a, b = train[:, :elements], train[:, elements:]
    left = jnp.concatenate([a, b], axis=0)
    right = jnp.concatenate([b, -a], axis=0)
    share = 1.0 / gates
    gram_re = mm(left, left, TN, None)
    gram_im = mm(right, left, TN, None)
    corner = lax.broadcasted_iota(jnp.int32, (elements, elements), 0) == lax.broadcasted_iota(
        jnp.int32, (elements, elements), 1
    )
    mat_re[:, :elements] = gram_re * share + jnp.where(corner, LOADING, 0.0)
    mat_im[:, :elements] = gram_im * share
    mat_re[:, elements:] = rhs_re_ref[...]
    mat_im[:, elements:] = rhs_im_ref[...]

    lane = lax.broadcasted_iota(jnp.int32, (BLOCK, BLOCK), 1)
    unit = jnp.where(lax.broadcasted_iota(jnp.int32, (BLOCK, BLOCK), 0) == lane, 1.0, 0.0)
    blank = jnp.zeros((BLOCK, BLOCK), jnp.float32)
    steps = elements // BLOCK
    for k in range(steps):
        at = k * BLOCK
        d_re = mat_re[at : at + BLOCK, at : at + BLOCK]
        d_im = mat_im[at : at + BLOCK, at : at + BLOCK]
        work = jnp.concatenate([d_re, d_im, unit, blank], axis=1)
        turned = jnp.concatenate([-d_im, d_re, blank, unit], axis=1)
        work, turned = eliminate(work, turned)
        emb = jnp.concatenate([turned[:, 2 * BLOCK :], work[:, 2 * BLOCK :]], axis=0)
        emb_ref[k] = emb
        left_lane = at // LANES * LANES
        rows_re = mat_re[at : at + BLOCK, left_lane:]
        rows_im = mat_im[at : at + BLOCK, left_lane:]
        solved = mm(emb, jnp.concatenate([rows_im, rows_re], axis=0), NN)
        mat_re[at : at + BLOCK, left_lane:] = solved[:BLOCK]
        mat_im[at : at + BLOCK, left_lane:] = solved[BLOCK:]
        if k + 1 < steps:
            nxt = at + BLOCK
            cross = jnp.concatenate([solved[BLOCK:], -solved[:BLOCK]], axis=0)
            stem = solved[:, : elements - left_lane]
            upd_re = mm(stem, solved, TN)
            upd_im = mm(stem, cross, TN)
            mat_re[nxt:, left_lane:] = mat_re[nxt:, left_lane:] - upd_re[nxt - left_lane :]
            mat_im[nxt:, left_lane:] = mat_im[nxt:, left_lane:] - upd_im[nxt - left_lane :]

    wts_ref[...] = jnp.zeros_like(wts_ref)
    used = lax.broadcasted_iota(jnp.int32, (BLOCK, LANES), 1) < 4
    for k in reversed(range(steps)):
        at = k * BLOCK
        v_re = mat_re[at : at + BLOCK, elements:]
        v_im = mat_im[at : at + BLOCK, elements:]
        if k + 1 < steps:
            first = (at + BLOCK) // LANES * LANES
            r_re = mat_re[at : at + BLOCK, first:elements]
            r_im = mat_im[at : at + BLOCK, first:elements]
            prod = mm(jnp.concatenate([r_re, r_im], axis=0), wts_ref[first:], NN)
            top, low = prod[:BLOCK], prod[BLOCK:]
            v_re = v_re - top + pltpu.roll(low, 64, 1)
            v_im = v_im - low - pltpu.roll(top, 64, 1)
        v = jnp.concatenate([jnp.where(used, v_re, 0.0), jnp.where(used, v_im, 0.0)], axis=0)
        w = mm(emb_ref[k], v, TN)
        wts_ref[at : at + BLOCK] = w[BLOCK:] + pltpu.roll(w[:BLOCK], 64, 1)

    wts = wts_ref[...]
    paired = rhs_re_ref[...] + pltpu.roll(rhs_im_ref[...], 64, 1)
    half = jnp.sum(paired * wts, axis=0, keepdims=True)
    response = half + pltpu.roll(half, 64, 1)
    wts = wts * jnp.where(response > 0.0, lax.rsqrt(response), 0.0)
    for ref, slot in ((own_ref, 1), (other_ref, 2)):
        at = pl.multiple_of(place_ref[slot] * gate_dev, 8)
        from_re = mm(wts, x_re[pl.ds(at, gate_dev)], ((0,), (1,)))
        from_im = mm(wts, x_im[pl.ds(at, gate_dev)], ((0,), (1,)))
        ref[0:8, :gate_dev] = from_re[0:8] + from_im[64:72]
        ref[8:16, :gate_dev] = from_im[0:8] - from_re[64:72]


def adapt(place, code, chunks, rhs_re, rhs_im):
    count, _, rows, elements = chunks.shape
    gate_dev = (rows - MASK_ROWS) // 2
    gates = count * gate_dev
    width = elements + LANES
    whole = lambda shape: pl.BlockSpec(shape, lambda i, p: (0,) * len(shape))
    f32 = jnp.float32
    return pl.pallas_call(
        adapt_kernel,
        grid_spec=pltpu.PrefetchScalarGridSpec(
            num_scalar_prefetch=1,
            grid=(1,),
            in_specs=[
                pl.BlockSpec(memory_space=pltpu.SMEM),
                pl.BlockSpec((count, 1, rows, elements), lambda i, p: (0, p[0], 0, 0)),
                whole((elements, LANES)),
                whole((elements, LANES)),
            ],
            out_specs=[whole((16, LANES)), whole((16, LANES))],
            scratch_shapes=[
                pltpu.VMEM((gates + 2 * HEAD, elements), f32),
                pltpu.VMEM((gates + 2 * HEAD, elements), f32),
                pltpu.VMEM((gates, elements), f32),
                pltpu.VMEM((gates, elements), f32),
                pltpu.VMEM((gates, 2 * elements), jnp.bfloat16),
                pltpu.VMEM((elements, width), f32),
                pltpu.VMEM((elements, width), f32),
                pltpu.VMEM((elements // BLOCK, 2 * BLOCK, 2 * BLOCK), f32),
                pltpu.VMEM((elements, LANES), f32),
            ],
        ),
        out_shape=[jax.ShapeDtypeStruct((16, LANES), f32)] * 2,
        name="adapt",
    )(place, code, chunks, rhs_re, rhs_im)


def steering_columns(steer_row, elements):
    element = jnp.arange(elements, dtype=jnp.int32)
    turn = jnp.mod(
        element[:, None] * (2 * steer_row[None, :] - elements), 2 * elements
    ).astype(jnp.float32)
    phases = turn * (math.pi / elements)
    pad = ((0, 0), (0, LANES - steer_row.shape[0]))
    return jnp.pad(jnp.cos(phases), pad), jnp.pad(jnp.sin(phases), pad)


def shards(raw_samples, filter_taps, range_code, train_mask, steer_index):
    elem_dev, gate_dev = raw_samples.shape[:2]
    bin_dev, beams = steer_index.shape
    dop_count, rng_count = lax.axis_size("dop"), lax.axis_size("rng")
    elements = elem_dev * dop_count
    bin_total = bin_dev * dop_count
    total = jnp.zeros((elem_dev, gate_dev, 2, CHANNELS), jnp.float32)
    for t in range(TAPS):
        piece = raw_samples[..., t * CHANNELS : (t + 1) * CHANNELS].astype(jnp.float32)
        total = total + piece * filter_taps[t]
    filtered = total.astype(jnp.bfloat16)
    rows = jnp.transpose(filtered, (2, 1, 0, 3)).reshape(2 * gate_dev * elem_dev, CHANNELS)
    parts = lax.dot_general(
        dft_columns(bin_total), rows, (((0,), (1,)), ((), ())), preferred_element_type=jnp.float32
    )
    cosine, sine = parts[:bin_total], parts[bin_total:]
    half = gate_dev * elem_dev
    spec_re = cosine[:, :half] + sine[:, half:]
    spec_im = cosine[:, half:] - sine[:, :half]
    spectra = jnp.concatenate([spec_re, spec_im], axis=1).astype(jnp.bfloat16)
    turned = lax.all_to_all(spectra, "dop", split_axis=0, concat_axis=0, tiled=True)
    turned = turned.reshape(dop_count, bin_dev, 2 * gate_dev, elem_dev)
    turned = jnp.transpose(turned, (1, 2, 0, 3)).reshape(bin_dev, 2 * gate_dev, elements)
    mask = jnp.pad(
        train_mask.astype(jnp.bfloat16)[:, None, :],
        ((0, 0), (0, MASK_ROWS - 1), (0, elements - gate_dev)),
    )
    chunk = jnp.concatenate([turned, mask], axis=1)
    chunks = lax.all_gather(chunk, "rng", axis=0, tiled=False)
    position = lax.axis_index("rng")
    core = position % bin_dev
    place = jnp.stack([core, position, position ^ 1]).astype(jnp.int32)
    steer_row = lax.dynamic_index_in_dim(steer_index, core, 0, keepdims=False)
    rhs_re, rhs_im = steering_columns(steer_row, elements)
    own, other = adapt(place, range_code, chunks, rhs_re, rhs_im)
    swapped = lax.ppermute(other, "rng", [(i, i ^ 1) for i in range(rng_count)])
    trim = lambda x: x.reshape(2, 8, LANES)[:, :beams, :gate_dev]
    own, swapped = trim(own), trim(swapped)
    low = jnp.where(core == 0, own, swapped)
    high = jnp.where(core == 0, swapped, own)
    return jnp.stack([low, high], axis=1)


def solution(mesh):
    return jax.shard_map(
        shards,
        mesh=mesh,
        in_specs=(P("dop", "rng", None, None), P(), P(), P("dop", "rng"), P("dop", None)),
        out_specs=P(None, "dop", None, "rng"),
        check_vma=False,
    )
```

time: 477 us -> 87 us (0.18); the launches traced: 470 us -> 86.8 us
  other arithmetic: 265 us -> 5.82 us
  waiting for transfers between devices: 123 us -> 7.19 us
  Pallas kernels: 0 us -> 27.8 us
  blocking collectives: 0 us -> 23.6 us
  local copies, waits for them, and re-layouts: 27.3 us -> 6.12 us
  matrix products: 19.7 us -> 0.29 us
  between operations: 14.3 us -> 0.2 us
  starting transfers between devices: 20.8 us -> 15.8 us
    another operation x24 -> x4, other arithmetic: 236 us -> 2.06 us  [the longest x2 1.31 us: shards(): return jnp.stack([low, high], axis=1)]
    psum x1 -> x0, waiting for transfers between devices: 112 us -> none  [shards(): symmetric, skewed = lax.psum((symmetric, skewed), 'rng')]
    pallas_call x0 -> x1, Pallas kernels: none -> 27.8 us  [adapt(): pl.pallas_call(adapt_kernel, grid_spec=pltpu.PrefetchScalarGridSpec(num_s...]
    all_gather x0 -> x1, blocking collectives: none -> 23.6 us  [shards(): chunks = lax.all_gather(chunk, 'rng', axis=0, tiled=False)]
    slice x2 -> x0, other arithmetic: 17.5 us -> none  [the longest x1 8.75 us: beam_output(): signal[:, :, 0]]
    another operation x20 -> x0, matrix products: 16.7 us -> none  [the longest x14 9.99 us: solve_all(): jax.scipy.linalg.cho_solve((lower_part, True), target)]
    another operation x17 -> x0, local copies, waits for them, and re-layouts: 14.9 us -> none
    reshape x3 -> x1, local copies, waits for them, and re-layouts: 6.73 us -> 0.09 us  [shards(): jnp.transpose(turned, (1, 2, 0, 3)).reshape(bin_dev, 2 * gate_dev, elements)]
  transfers between devices with their start and end apart: 4 -> 2, of which waited for: 3 -> 2; matrix products, arithmetic and copies ran while one was open for 0% -> 3% of each run, Pallas kernels for 0% -> 0%
where the time goes in v1:
time: 87 us; the launch traced here: 86.8 us
  Pallas kernels  27.8 us (32%)
  blocking collectives  23.6 us (27%)
  starting transfers between devices  15.8 us (18%)
  waiting for transfers between devices  7.19 us (8%)
  local copies, waits for them, and re-layouts  6.12 us (7%)
  other arithmetic  5.82 us (7%)
    pallas_call x1, Pallas kernels, adapt(): pl.pallas_call(adapt_kernel, grid_spec=pltpu.PrefetchScalarGridSpec(num_s...  27.8 us
    all_gather x1, blocking collectives, shards(): chunks = lax.all_gather(chunk, 'rng', axis=0, tiled=False)  23.6 us
    all_to_all x1, starting transfers between devices, shards(): lax.all_to_all(spectra, 'dop', split_axis=0, concat_axis=0, tiled=True)  13.7 us
    all_to_all x1, waiting for transfers between devices, shards(): lax.all_to_all(spectra, 'dop', split_axis=0, concat_axis=0, tiled=True)  5.99 us
    slice x1, local copies, waits for them, and re-layouts, shards(): raw_samples[..., t * CHANNELS:(t + 1) * CHANNELS].astype(jnp.float32)  4.11 us
    convert_element_type x1, other arithmetic, shards(): filtered = total.astype(jnp.bfloat16)  2.48 us
    ppermute x1, starting transfers between devices, shards(): swapped = lax.ppermute(other, 'rng', [(i, i ^ 1) for i in range(rng_count)])  2.06 us
  transfers between devices with their start and end apart: 2, of which 2 were waited for; matrix products, arithmetic and copies ran while one was open for 3% of the time, Pallas kernels for 0%

profile of v1, /device:TPU:1, one launch (start us, length us, event | category | flops | bytes accessed | tf_op | source)
XLA Modules:
  0.0 86.8 jit_solution(6726206928271161087)
XLA Ops:
  0.0 4.1 %fusion.6 = (bf16[8,24,2,512]{3,2,1,0:T(2,128)(2,1)S(1)}, bf16[8,24,2,512]{3,2,1,0:T(2,128)(2,1)S(1)}, bf16[8,24,2,512]{3,2,1,0:T(2,128)(2,1)S(1)}, bf16[8,24,2,...) fusion(bf16[8,24,2,4096]{3,2,1,0:T(2,128)(2,1)} %param.6), kind=kLoop, calls=%fused_computation.22 | loop fusion | bytes 6291456 | tf_op jit(solution)/shard_map/slice | solution.py:260
  4.1 0.0 copy-start
  4.2 0.0 copy-start.3
  4.2 2.5 %add_convert_fusion = bf16[8,24,2,512]{3,0,1,2:T(8,128)(2,1)S(1)} fusion(bf16[8,24,2,512]{3,2,1,0:T(2,128)(2,1)S(1)} %get-tuple-element.16, bf16[8,24,2,512]{3,2,1,0:T(2,128)(2,1)S(1)} %get-tuple-element.10, bf16[8,24,2,512]{3,2,1,0:T(2,128)(2,1)S(1)} %get-tuple-element.11, bf16[8,24,2,512]{3,2,1,0:T(2,128)(2,1)S(1)} %get-tuple-element.12, ...), kind=kLoop, calls=%fused_computation | loop fusion | flops 4718592 | bytes 3555328 | tf_op jit(solution)/shard_map/convert_element_type | solution.py:262
  6.7 0.3 fusion.8
  7.0 0.1 fusion.2
  7.1 0.7 pad_maximum_fusion
  7.9 13.7 %all-to-all-start = ((bf16[32,2,384]{2,1,0:T(2,128)(2,1)}), bf16[32,2,384]{2,1,0:T(2,128)(2,1)S(1)}, u32[]{:S(2)}, u32[]{:S(2)}) async-start(bf16[32,2,384]{2,1,0:T(2,128)(2,1)} %pad_maximum_fusion), calls=%async_computation | async-start | bytes 98304 | tf_op jit(solution)/shard_map/all_to_all | solution.py:272
  21.6 0.1 fusion.5
  21.7 0.1 copy.65
  21.9 0.5 multiply_sine_fusion
  22.3 0.7 pad.12.rhs_re_ref
  23.0 0.7 pad.13.rhs_im_ref
  23.7 0.6 pad_add_fusion.place_ref
  24.3 6.0 %all-to-all-done = bf16[32,2,384]{2,1,0:T(2,128)(2,1)S(1)} async-done(((bf16[32,2,384]{2,1,0:T(2,128)(2,1)}), bf16[32,2,384]{2,1,0:T(2,128)(2,1)S(1)}, u32[]{:S(2)}, u32[]{:S(2)}) %all-to-all-start) | async-done | bytes 49184 | tf_op jit(solution)/shard_map/all_to_all | solution.py:272
  30.3 0.2 copy.61
  30.5 0.2 copy.62
  30.7 0.1 copy.63
  30.8 23.6 %all-gather = bf16[32,56,256]{2,1,0:T(8,128)(2,1)} all-gather(bf16[2,56,256]{2,1,0:T(8,128)(2,1)S(1)} %fusion.3), channel_id=2, replica_groups=mesh['dop'=32,'rng'=16] {'rng'}, dimensions={0}, use_global_device_ids=true | all-gather | bytes 974848 | tf_op jit(solution)/shard_map/all_gather | solution.py:280
  54.4 27.8 %adapt.1 = (f32[16,128]{1,0:T(8,128)}, f32[16,128]{1,0:T(8,128)}) custom-call(s32[3]{0:T(128)} %pad_add_fusion.place_ref, f32[2,7]{1,0:T(2,128)} %code_ref.1, bf16[16,2,56,256]{3,2,1,0:T(8,128)(2,1)} %bitcast.33, f32[256,128]{1,0:T(8,128)} %pad.12.rhs_re_ref, f32[256,128]{1,0:T(8,128)} %pad.13.rhs_im_ref), custom_call_target="tpu_custom_call" | custom-call | tf_op jit(solution)/shard_map/adapt/pallas_call | solution.py:213
  82.2 2.1 %collective-permute-start = (f32[16,128]{1,0:T(8,128)}, f32[16,128]{1,0:T(8,128)S(1)}, u32[]{:S(2)}, u32[]{:S(2)}) collective-permute-start(f32[16,128]{1,0:T(8,128)} %get-tuple-element.8), channel_id=1, source_target_pairs={{0,1},{1,0},{2,3},{3,2},{4,5},{5,4},{6,7},{7,6},{8,9},{9,8},{10,11... | collective-permute-start | bytes 24584 | tf_op jit(solution)/shard_map/ppermute | solution.py:287
  84.3 1.2 %collective-permute-done = f32[16,128]{1,0:T(8,128)S(1)} collective-permute-done((f32[16,128]{1,0:T(8,128)}, f32[16,128]{1,0:T(8,128)S(1)}, u32[]{:S(2)}, u32[]{:S(2)}) %collective-permute-start) | collective-permute-done | bytes 8224 | tf_op jit(solution)/shard_map/ppermute | solution.py:287
  85.5 0.7 select_bitcast_fusion.1
  86.2 0.6 pad_maximum_fusion.1
  (13 shorter events, 0.1 us)
Async XLA Ops:
  0.0 4.1 %copy-start.1 = (f32[8,512]{1,0:T(8,128)S(1)}, f32[8,512]{1,0:T(8,128)}, u32[]{:S(2)}) copy-start(f32[8,512]{1,0:T(8,128)} %param.7) | copy-start | bytes 49156
  4.1 2.5 %copy-start = (bf16[512,128]{1,0:T(8,128)(2,1)S(1)}, bf16[512,128]{1,0:T(8,128)(2,1)}, u32[]{:S(2)}) copy-start(bf16[512,128]{1,0:T(8,128)(2,1)} %constant.49.clone) | copy-start | bytes 393220
  4.1 17.4 %copy-start.2 = (s32[2,24]{1,0:T(2,128)S(1)}, s32[2,24]{1,0:T(2,128)}, u32[]{:S(2)}) copy-start(s32[2,24]{1,0:T(2,128)} %param.9) | copy-start | bytes 580
  4.2 17.5 %copy-start.3 = (s32[2,4]{1,0:T(2,128)S(1)}, s32[2,4]{1,0:T(2,128)}, u32[]{:S(2)}) copy-start(s32[2,4]{1,0:T(2,128)} %param.10) | copy-start | bytes 100
  7.9 22.4 %all-to-all-start = ((bf16[32,2,384]{2,1,0:T(2,128)(2,1)}), bf16[32,2,384]{2,1,0:T(2,128)(2,1)S(1)}, u32[]{:S(2)}, u32[]{:S(2)}) async-start(bf16[32,2,384]{2,1,0:T(2,128)(2,1)} %pad_maximum_fusion), calls=%async_computation | async-start | bytes 98304 | tf_op jit(solution)/shard_map/all_to_all | solution.py:272
  82.2 3.3 %collective-permute-start = (f32[16,128]{1,0:T(8,128)}, f32[16,128]{1,0:T(8,128)S(1)}, u32[]{:S(2)}, u32[]{:S(2)}) collective-permute-start(f32[16,128]{1,0:T(8,128)} %get-tuple-element.8), channel_id=1, source_target_pairs={{0,1},{1,0},{2,3},{3,2},{4,5},{5,4},{6,7},{7,6},{8,9},{9,8},{10,11... | collective-permute-start | bytes 24584 | tf_op jit(solution)/shard_map/ppermute | solution.py:287

commit v2 on v1

v2 whole, which is shorter than its diff:
```python
import math

import jax
import jax.numpy as jnp
import numpy as np
from jax import lax
from jax.experimental import pallas as pl
from jax.experimental.pallas import tpu as pltpu
from jax.sharding import PartitionSpec as P

CHANNELS = 512
TAPS = 8
CODE_REACH = 3
LOADING = 0.25
BLOCK = 32
STEP = 4
LANES = 128
HEAD = 8
TILE = 96
MASK_ROWS = 8

HIGHEST = lax.Precision.HIGHEST


def dft_rows(bin_total):
    mode = np.arange(CHANNELS, dtype=np.int64)[None, :]
    turn = (mode * np.arange(bin_total, dtype=np.int64)[:, None]) % CHANNELS
    phases = turn.astype(np.float32) * np.float32(2.0 * math.pi / CHANNELS)
    scale = np.float32(math.sqrt(CHANNELS))
    both = np.concatenate([np.cos(phases) / scale, np.sin(phases) / scale], axis=0)
    return jnp.asarray(both, jnp.bfloat16)


def mm(a, b, dims, precision=HIGHEST):
    return lax.dot_general(
        a, b, (dims, ((), ())), precision=precision, preferred_element_type=jnp.float32
    )


NN = ((1,), (0,))
TN = ((0,), (0,))
NT = ((1,), (1,))


def eliminate(work, turned):
    rows = lax.broadcasted_iota(jnp.int32, work.shape, 0)
    scale = jnp.zeros_like(work)
    for base in range(0, BLOCK, STEP):
        col_re = [jnp.broadcast_to(work[:, base + t : base + t + 1], work.shape) for t in range(STEP)]
        col_im = [
            jnp.broadcast_to(work[:, BLOCK + base + t : BLOCK + base + t + 1], work.shape)
            for t in range(STEP)
        ]
        for t in range(STEP):
            j = base + t
            pivot = jnp.broadcast_to(col_re[t][j : j + 1], (8, LANES))
            inverse = jnp.concatenate([1.0 / pivot] * (BLOCK // 8), axis=0)
            below = rows > j
            m_re = jnp.where(below, col_re[t] * inverse, 0.0)
            m_im = jnp.where(below, col_im[t] * inverse, 0.0)
            for u in range(t + 1, STEP):
                e_re = jnp.broadcast_to(col_re[u][j : j + 1], work.shape)
                e_im = jnp.broadcast_to(col_im[u][j : j + 1], work.shape)
                col_re[u], col_im[u] = (
                    col_re[u] - m_re * e_re + m_im * e_im,
                    col_im[u] - m_re * e_im - m_im * e_re,
                )
            row = jnp.broadcast_to(work[j : j + 1], work.shape)
            row_turned = jnp.broadcast_to(turned[j : j + 1], work.shape)
            work, turned = (
                work - m_re * row - m_im * row_turned,
                turned - m_re * row_turned + m_im * row,
            )
            scale = jnp.where(rows == j, inverse, scale)
    return work * jnp.sqrt(scale)


def split3(x):
    high = x.astype(jnp.bfloat16)
    rest = x - high.astype(jnp.float32)
    mid = rest.astype(jnp.bfloat16)
    low = (rest - mid.astype(jnp.float32)).astype(jnp.bfloat16)
    return high, mid, low


def dot6(left, right):
    high, mid, low = left
    count = high.shape[0]
    first = mm(jnp.concatenate([high, mid, low], axis=0), right[0], NN, None)
    second = mm(jnp.concatenate([high, mid], axis=0), right[1], NN, None)
    third = mm(high, right[2], NN, None)
    small = first[2 * count :] + second[count:] + third
    return first[:count] + (first[count : 2 * count] + second[:count] + small)


def stack_turned(x, elements, sign):
    lane = lax.broadcasted_iota(jnp.int32, (x.shape[0], LANES), 1)
    tail = pltpu.roll(x[:, 2 * elements :], 64, 1)
    tail = jnp.where((lane < 64) == (sign > 0), -tail, tail)
    out = []
    for whole, end in zip(split3(x), split3(tail)):
        real, imag = whole[:, :elements], whole[:, elements : 2 * elements]
        real, imag = (-imag, real) if sign > 0 else (imag, -real)
        out.append(jnp.concatenate([whole, jnp.concatenate([real, imag, end], axis=1)], axis=0))
    return out


def adapt_kernel(
    place_ref,
    code_ref,
    chunks_ref,
    steer_re_ref,
    steer_im_ref,
    own_ref,
    other_ref,
    sig_re,
    sig_im,
    x_re,
    x_im,
    train,
    mat,
    v_high,
    v_mid,
    v_low,
    s_high,
    s_mid,
    s_low,
):
    chunk_count, _, _, elements = chunks_ref.shape
    gate_dev = (chunks_ref.shape[2] - MASK_ROWS) // 2
    gates = chunk_count * gate_dev
    f32, bf16 = jnp.float32, jnp.bfloat16
    for ref in (sig_re, sig_im):
        ref[0:HEAD] = jnp.zeros((HEAD, elements), f32)
        ref[HEAD + gates :] = jnp.zeros((ref.shape[0] - HEAD - gates, elements), f32)
    diagonal = lax.broadcasted_iota(jnp.int32, (gate_dev, LANES), 0) == lax.broadcasted_iota(
        jnp.int32, (gate_dev, LANES), 1
    )
    masks = []
    for c in range(chunk_count):
        chunk = chunks_ref[c, 0].astype(f32)
        at = HEAD + c * gate_dev
        sig_re[at : at + gate_dev] = chunk[:gate_dev]
        sig_im[at : at + gate_dev] = chunk[gate_dev : 2 * gate_dev]
        mask_row = chunk[2 * gate_dev : 2 * gate_dev + 1, :LANES]
        masks.append(jnp.sum(jnp.where(diagonal, mask_row, 0.0), axis=1, keepdims=True))

    tap = (
        lax.broadcasted_iota(jnp.int32, (TILE, LANES), 1)
        - lax.broadcasted_iota(jnp.int32, (TILE, LANES), 0)
        - (HEAD - CODE_REACH)
    )
    band_re = jnp.zeros((TILE, LANES), f32)
    band_im = jnp.zeros((TILE, LANES), f32)
    for t in range(2 * CODE_REACH + 1):
        band_re = jnp.where(tap == t, code_ref[0, t], band_re)
        band_im = jnp.where(tap == t, code_ref[1, t], band_im)
    band = jnp.concatenate(
        [
            jnp.concatenate([band_re, -band_im], axis=1),
            jnp.concatenate([band_im, band_re], axis=1),
        ],
        axis=0,
    )
    bands = split3(band)
    for c in range(gates // TILE):
        at = c * TILE
        window = jnp.concatenate(
            [sig_re[at : at + LANES].astype(bf16), sig_im[at : at + LANES].astype(bf16)], axis=0
        )
        high, mid, low = (mm(part, window, NN, None) for part in bands)
        both = (high + (mid + low)).astype(bf16).astype(f32)
        real, imag = both[:TILE], both[TILE:]
        x_re[at : at + TILE] = real
        x_im[at : at + TILE] = imag
        per = TILE // gate_dev
        mask = jnp.concatenate(masks[c * per : (c + 1) * per], axis=0)
        train[at : at + TILE, :elements] = (real * mask).astype(bf16)
        train[at : at + TILE, elements:] = (imag * mask).astype(bf16)

    a, b = train[:, :elements], train[:, elements:]
    left = jnp.concatenate([a, b], axis=0)
    right = jnp.concatenate([jnp.concatenate([a, -b], axis=1), jnp.concatenate([b, a], axis=1)], axis=0)
    gram = mm(left, right, TN, None) * (1.0 / gates)
    corner = lax.broadcasted_iota(jnp.int32, (elements, elements), 0) == lax.broadcasted_iota(
        jnp.int32, (elements, elements), 1
    )
    mat[:, :elements] = gram[:, :elements] + jnp.where(corner, LOADING, 0.0)
    mat[:, elements : 2 * elements] = gram[:, elements:]

    spare = jnp.zeros((64 - 8 - 2 * gate_dev, elements), f32)
    sides = []
    for steer_ref, ref in ((steer_re_ref, x_re), (steer_im_ref, x_im)):
        sides.append(steer_ref[...])
        for slot in (1, 2):
            at = pl.multiple_of(place_ref[slot] * gate_dev, 8)
            sides.append(ref[pl.ds(at, gate_dev)])
        sides.append(spare)
    mat[:, 2 * elements :] = jnp.concatenate(sides, axis=0).T

    lane = lax.broadcasted_iota(jnp.int32, (BLOCK, BLOCK), 1)
    unit = jnp.where(lax.broadcasted_iota(jnp.int32, (BLOCK, BLOCK), 0) == lane, 1.0, 0.0)
    blank = jnp.zeros((BLOCK, BLOCK), f32)
    steps = elements // BLOCK
    acc = mat[0:BLOCK]
    for k in range(steps):
        at, nxt = k * BLOCK, (k + 1) * BLOCK
        seen = 2 * at
        d_re = acc[:, at:nxt]
        d_im = acc[:, elements + at : elements + nxt]
        panel = stack_turned(acc, elements, 1)
        if k + 1 < steps:
            later = mat[nxt : nxt + BLOCK]
            if k > 0:
                later = later - dot6(
                    [ref[nxt : nxt + BLOCK, :seen] for ref in (s_high, s_mid, s_low)],
                    [ref[:seen] for ref in (v_high, v_mid, v_low)],
                )
        work = jnp.concatenate([d_re, d_im, unit, blank], axis=1)
        turned = jnp.concatenate([-d_im, d_re, blank, unit], axis=1)
        work = eliminate(work, turned)
        solved = dot6(split3(work[:, 2 * BLOCK :]), panel)
        mat[at:nxt, 2 * elements :] = solved[:, 2 * elements :]
        if k + 1 < steps:
            trail = stack_turned(solved, elements, -1)
            first = nxt // LANES * LANES
            stem = jnp.concatenate(
                [solved[:, first:elements], solved[:, elements + first : 2 * elements]], axis=0
            ).T
            stems = split3(stem[nxt - first :])
            acc = later - dot6([part[:BLOCK] for part in stems], trail)
            for ref, part in zip((v_high, v_mid, v_low), trail):
                ref[seen : seen + 2 * BLOCK] = part
            for ref, part in zip((s_high, s_mid, s_low), stems):
                ref[nxt:, seen : seen + 2 * BLOCK] = part

    whitened = mat[:, 2 * elements :]
    inner = mm(whitened, whitened, TN)
    top, low = inner[0:8], pltpu.roll(inner[64:72], 64, 1)
    real = top + low
    imag = pltpu.roll(top - low, 64, 1)
    own_lane = lax.broadcasted_iota(jnp.int32, (8, LANES), 1) == lax.broadcasted_iota(
        jnp.int32, (8, LANES), 0
    )
    response = jnp.sum(jnp.where(own_lane, real, 0.0), axis=1, keepdims=True)
    factor = lax.rsqrt(jnp.where(response > 0.0, response, 1.0))
    both = jnp.concatenate([real * factor, imag * factor], axis=0)
    own_ref[...] = pltpu.roll(both, LANES - 8, 1)
    other_ref[...] = pltpu.roll(both, LANES - 8 - gate_dev, 1)


def adapt(place, code, chunks, steer_re, steer_im):
    count, _, rows, elements = chunks.shape
    gate_dev = (rows - MASK_ROWS) // 2
    gates = count * gate_dev
    width = 2 * elements + LANES
    whole = lambda shape: pl.BlockSpec(shape, lambda i, p: (0,) * len(shape))
    f32, bf16 = jnp.float32, jnp.bfloat16
    return pl.pallas_call(
        adapt_kernel,
        grid_spec=pltpu.PrefetchScalarGridSpec(
            num_scalar_prefetch=1,
            grid=(1,),
            in_specs=[
                pl.BlockSpec(memory_space=pltpu.SMEM),
                pl.BlockSpec((count, 1, rows, elements), lambda i, p: (0, p[0], 0, 0)),
                whole((8, elements)),
                whole((8, elements)),
            ],
            out_specs=[whole((16, LANES)), whole((16, LANES))],
            scratch_shapes=[
                pltpu.VMEM((gates - TILE + LANES + HEAD, elements), f32),
                pltpu.VMEM((gates - TILE + LANES + HEAD, elements), f32),
                pltpu.VMEM((gates, elements), f32),
                pltpu.VMEM((gates, elements), f32),
                pltpu.VMEM((gates, 2 * elements), bf16),
                pltpu.VMEM((elements, width), f32),
            ]
            + [pltpu.VMEM((2 * elements, width), bf16)] * 3
            + [pltpu.VMEM((elements, 2 * elements), bf16)] * 3,
        ),
        out_shape=[jax.ShapeDtypeStruct((16, LANES), f32)] * 2,
        name="adapt",
    )(place, code, chunks, steer_re, steer_im)


def channel_kernel(raw_ref, taps_ref, table_ref, out_ref, filtered):
    step = pl.program_id(0)
    elem_dev = pl.num_programs(0)
    rows = out_ref.shape[1] // 2
    gate_dev = rows // 8
    weights = [taps_ref[t] for t in range(TAPS)]
    for g in range(gate_dev):
        at = g * 8 * TAPS
        piece = raw_ref[at : at + 8 * TAPS].astype(jnp.float32)
        total = piece[0:8] * weights[0]
        for t in range(1, TAPS):
            total = total + piece[8 * t : 8 * t + 8] * weights[t]
        to = pl.multiple_of((g * elem_dev + step) * 8, 8)
        filtered[pl.ds(to, 8)] = total.astype(jnp.bfloat16).astype(jnp.float32)

    @pl.when(step == elem_dev - 1)
    def _():
        sums = []
        for r in range(2):
            rows_r = jnp.concatenate(
                [filtered[pl.ds(2 * j + r, rows, stride=8)] for j in range(4)], axis=1
            ).astype(jnp.bfloat16)
            sums.append(mm(table_ref[...], rows_r, NT, None))
        half = out_ref.shape[0]
        re = sums[0][:half] + sums[1][half:]
        im = sums[1][:half] - sums[0][half:]
        out_ref[...] = jnp.concatenate([re, im], axis=1).astype(jnp.bfloat16)


def channelize(raw_samples, filter_taps, bin_total):
    elem_dev, gate_dev = raw_samples.shape[:2]
    tiles = CHANNELS // LANES
    flat = raw_samples.reshape(elem_dev, gate_dev, 2, TAPS * tiles, LANES)
    flat = jnp.transpose(flat, (0, 1, 3, 2, 4)).reshape(-1, LANES)
    taps = jnp.repeat(filter_taps.reshape(TAPS, tiles, 1, LANES), 2, axis=2).reshape(TAPS, 8, LANES)
    rows = gate_dev * elem_dev
    return pl.pallas_call(
        channel_kernel,
        grid=(elem_dev,),
        in_specs=[
            pl.BlockSpec((gate_dev * TAPS * tiles * 2, LANES), lambda e: (e, 0)),
            pl.BlockSpec((TAPS, 8, LANES), lambda e: (0, 0, 0)),
            pl.BlockSpec((2 * bin_total, CHANNELS), lambda e: (0, 0)),
        ],
        out_specs=pl.BlockSpec((bin_total, 2 * rows), lambda e: (0, 0)),
        out_shape=jax.ShapeDtypeStruct((bin_total, 2 * rows), jnp.bfloat16),
        scratch_shapes=[pltpu.VMEM((rows * 8, LANES), jnp.float32)],
        name="channelize",
    )(flat, taps, dft_rows(bin_total))


def steering_rows(steer_row, elements):
    element = jnp.arange(elements, dtype=jnp.int32)
    turn = jnp.mod(
        element[None, :] * (2 * steer_row[:, None] - elements), 2 * elements
    ).astype(jnp.float32)
    phases = turn * (math.pi / elements)
    pad = ((0, 8 - steer_row.shape[0]), (0, 0))
    return jnp.pad(jnp.cos(phases), pad), jnp.pad(jnp.sin(phases), pad)


def shards(raw_samples, filter_taps, range_code, train_mask, steer_index):
    elem_dev, gate_dev = raw_samples.shape[:2]
    bin_dev, beams = steer_index.shape
    dop_count, rng_count = lax.axis_size("dop"), lax.axis_size("rng")
    elements = elem_dev * dop_count
    bin_total = bin_dev * dop_count
    spectra = channelize(raw_samples, filter_taps, bin_total)
    turned = lax.all_to_all(spectra, "dop", split_axis=0, concat_axis=0, tiled=True)
    turned = turned.reshape(dop_count, bin_dev, 2 * gate_dev, elem_dev)
    turned = jnp.transpose(turned, (1, 2, 0, 3)).reshape(bin_dev, 2 * gate_dev, elements)
    mask = jnp.pad(
        train_mask.astype(jnp.bfloat16)[:, None, :],
        ((0, 0), (0, MASK_ROWS - 1), (0, elements - gate_dev)),
    )
    chunk = jnp.concatenate([turned, mask], axis=1)
    chunks = lax.all_gather(chunk, "rng", axis=0, tiled=False)
    position = lax.axis_index("rng")
    core = position % bin_dev
    place = jnp.stack([core, position, position ^ 1]).astype(jnp.int32)
    steer_row = lax.dynamic_index_in_dim(steer_index, core, 0, keepdims=False)
    steer_re, steer_im = steering_rows(steer_row, elements)
    own, other = adapt(place, range_code, chunks, steer_re, steer_im)
    swapped = lax.ppermute(other, "rng", [(i, i ^ 1) for i in range(rng_count)])
    trim = lambda x: x.reshape(2, 8, LANES)[:, :beams, :gate_dev]
    own, swapped = trim(own), trim(swapped)
    low = jnp.where(core == 0, own, swapped)
    high = jnp.where(core == 0, swapped, own)
    return jnp.stack([low, high], axis=1)


def solution(mesh):
    return jax.shard_map(
        shards,
        mesh=mesh,
        in_specs=(P("dop", "rng", None, None), P(), P(), P("dop", "rng"), P("dop", None)),
        out_specs=P(None, "dop", None, "rng"),
        check_vma=False,
    )
```

time: 87 us -> 79.7 us (0.916)
  other arithmetic: 5.82 us -> 2.01 us
  Pallas kernels: 27.8 us -> 25.5 us
  local copies, waits for them, and re-layouts: 6.12 us -> 4.47 us
    pallas_call x1, Pallas kernels: 27.8 us -> 19.9 us  [adapt(): pl.pallas_call(adapt_kernel, grid_spec=pltpu.PrefetchScalarGridSpec(num_s...]
    pallas_call x0 -> x1, Pallas kernels: none -> 5.61 us  [channelize(): pl.pallas_call(channel_kernel, grid=(elem_dev,), in_specs=[pl.BlockSpec((...]
    slice x2 -> x0, local copies, waits for them, and re-layouts: 4.13 us -> none  [the longest x1 4.11 us: shards(): raw_samples[..., t * CHANNELS:(t + 1) * CHANNELS].astype(jnp.float32)]
    convert_element_type x2 -> x0, other arithmetic: 2.55 us -> none  [the longest x1 2.48 us: shards(): filtered = total.astype(jnp.bfloat16)]
    all_to_all x1 -> x2, local copies, waits for them, and re-layouts: 0.18 us -> 1.62 us  [shards(): lax.all_to_all(spectra, 'dop', split_axis=0, concat_axis=0, tiled=True)]
  transfers between devices with their start and end apart: 2 -> 2, of which waited for: 2 -> 2; matrix products, arithmetic and copies ran while one was open for 3% -> 2% of each run, Pallas kernels for 0% -> 0%
where the time goes in v2:
time: 79.7 us; the launch traced here: 79.3 us
  Pallas kernels  25.5 us (32%)
  blocking collectives  23.4 us (29%)
  starting transfers between devices  15.8 us (20%)
  waiting for transfers between devices  7.98 us (10%)
  local copies, waits for them, and re-layouts  4.47 us (6%)
  other arithmetic  2.01 us (3%)
    all_gather x1, blocking collectives, shards(): chunks = lax.all_gather(chunk, 'rng', axis=0, tiled=False)  23.4 us
    pallas_call x1, Pallas kernels, adapt(): pl.pallas_call(adapt_kernel, grid_spec=pltpu.PrefetchScalarGridSpec(num_s...  19.9 us
    all_to_all x1, starting transfers between devices, shards(): lax.all_to_all(spectra, 'dop', split_axis=0, concat_axis=0, tiled=True)  13.7 us
    all_to_all x1, waiting for transfers between devices, shards(): lax.all_to_all(spectra, 'dop', split_axis=0, concat_axis=0, tiled=True)  6.77 us
    pallas_call x1, Pallas kernels, channelize(): pl.pallas_call(channel_kernel, grid=(elem_dev,), in_specs=[pl.BlockSpec((...  5.61 us
    ppermute x1, starting transfers between devices, shards(): swapped = lax.ppermute(other, 'rng', [(i, i ^ 1) for i in range(rng_count)])  2.05 us
    all_to_all x2, local copies, waits for them, and re-layouts, shards(): lax.all_to_all(spectra, 'dop', split_axis=0, concat_axis=0, tiled=True)  1.62 us
  transfers between devices with their start and end apart: 2, of which 2 were waited for; matrix products, arithmetic and copies ran while one was open for 2% of the time, Pallas kernels for 0%

profile of v2, /device:TPU:1, one launch (start us, length us, event | category | flops | bytes accessed | tf_op | source)
XLA Modules:
  0.0 79.3 jit_solution(1792820674455724067)
XLA Ops:
  0.0 0.0 copy-start
  0.0 0.0 copy-start.1
  0.0 0.7 copy.20
  0.8 0.6 broadcast_in_dim.8
  1.4 5.6 %channelize.1 = bf16[64,384]{1,0:T(8,128)(2,1)} custom-call(bf16[12288,128]{1,0:T(8,128)(2,1)} %bitcast.28, f32[8,8,128]{2,1,0:T(8,128)} %bitcast.31, bf16[128,512]{1,0:T(8,128)(2,1)} %constant.49.clone.table_ref), custom_call_target="tpu_custom_call" | custom-call | tf_op jit(solution)/shard_map/channelize/pallas_call | solution.py:323
  7.0 1.4 %all_to_all.6 = bf16[32,2,384]{2,1,0:T(2,128)(2,1)} reshape(bf16[64,384]{1,0:T(8,128)(2,1)} %channelize.1) | data formatting | bytes 98304 | tf_op jit(solution)/shard_map/all_to_all | solution.py:355
  8.4 13.7 %all-to-all-start = ((bf16[32,2,384]{2,1,0:T(2,128)(2,1)}), bf16[32,2,384]{2,1,0:T(2,128)(2,1)S(1)}, u32[]{:S(2)}, u32[]{:S(2)}) async-start(bf16[32,2,384]{2,1,0:T(2,128)(2,1)} %all_to_all.6), calls=%async_computation | async-start | bytes 98304 | tf_op jit(solution)/shard_map/all_to_all | solution.py:355
  22.1 0.0 copy-done
  22.2 0.0 copy-done.1
  22.2 0.1 fusion.5
  22.3 0.6 pad.12.steer_re_ref
  22.9 0.6 pad.13.steer_im_ref
  23.5 0.6 pad_add_fusion.place_ref
  24.1 6.8 %all-to-all-done = bf16[32,2,384]{2,1,0:T(2,128)(2,1)S(1)} async-done(((bf16[32,2,384]{2,1,0:T(2,128)(2,1)}), bf16[32,2,384]{2,1,0:T(2,128)(2,1)S(1)}, u32[]{:S(2)}, u32[]{:S(2)}) %all-to-all-start) | async-done | bytes 49184 | tf_op jit(solution)/shard_map/all_to_all | solution.py:355
  30.9 0.2 copy.21
  31.0 0.2 copy.22
  31.2 0.1 copy.23
  31.4 23.4 %all-gather = bf16[32,56,256]{2,1,0:T(8,128)(2,1)} all-gather(bf16[2,56,256]{2,1,0:T(8,128)(2,1)S(1)} %fusion.1), channel_id=2, replica_groups=mesh['dop'=32,'rng'=16] {'rng'}, dimensions={0}, use_global_device_ids=true | all-gather | bytes 974848 | tf_op jit(solution)/shard_map/all_gather | solution.py:363
  54.8 19.9 %adapt.1 = (f32[16,128]{1,0:T(8,128)}, f32[16,128]{1,0:T(8,128)}) custom-call(s32[3]{0:T(128)} %pad_add_fusion.place_ref, f32[2,7]{1,0:T(2,128)} %code_ref.1, bf16[16,2,56,256]{3,2,1,0:T(8,128)(2,1)} %bitcast.27, f32[8,256]{1,0:T(8,128)} %pad.12.steer_re_ref, f32[8,256]{1,0:T(8,128)} %pad.13.steer_im_ref), custom_call_target="tpu_custom_call" | custom-call | tf_op jit(solution)/shard_map/adapt/pallas_call | solution.py:259
  74.7 2.0 %collective-permute-start = (f32[16,128]{1,0:T(8,128)}, f32[16,128]{1,0:T(8,128)S(1)}, u32[]{:S(2)}, u32[]{:S(2)}) collective-permute-start(f32[16,128]{1,0:T(8,128)} %get-tuple-element.8), channel_id=1, source_target_pairs={{0,1},{1,0},{2,3},{3,2},{4,5},{5,4},{6,7},{7,6},{8,9},{9,8},{10,11... | collective-permute-start | bytes 24584 | tf_op jit(solution)/shard_map/ppermute | solution.py:370
  76.7 1.2 %collective-permute-done = f32[16,128]{1,0:T(8,128)S(1)} collective-permute-done((f32[16,128]{1,0:T(8,128)}, f32[16,128]{1,0:T(8,128)S(1)}, u32[]{:S(2)}, u32[]{:S(2)}) %collective-permute-start) | collective-permute-done | bytes 8224 | tf_op jit(solution)/shard_map/ppermute | solution.py:370
  77.9 0.7 select_bitcast_fusion.1
  78.6 0.6 pad_maximum_fusion
  (4 shorter events, 0.0 us)
Async XLA Ops:
  0.0 22.1 %copy-start = (s32[2,24]{1,0:T(2,128)S(1)}, s32[2,24]{1,0:T(2,128)}, u32[]{:S(2)}) copy-start(s32[2,24]{1,0:T(2,128)} %param.9) | copy-start | bytes 580
  0.0 22.2 %copy-start.1 = (s32[2,4]{1,0:T(2,128)S(1)}, s32[2,4]{1,0:T(2,128)}, u32[]{:S(2)}) copy-start(s32[2,4]{1,0:T(2,128)} %param.10) | copy-start | bytes 100
  8.4 22.4 %all-to-all-start = ((bf16[32,2,384]{2,1,0:T(2,128)(2,1)}), bf16[32,2,384]{2,1,0:T(2,128)(2,1)S(1)}, u32[]{:S(2)}, u32[]{:S(2)}) async-start(bf16[32,2,384]{2,1,0:T(2,128)(2,1)} %all_to_all.6), calls=%async_computation | async-start | bytes 98304 | tf_op jit(solution)/shard_map/all_to_all | solution.py:355
  74.7 3.3 %collective-permute-start = (f32[16,128]{1,0:T(8,128)}, f32[16,128]{1,0:T(8,128)S(1)}, u32[]{:S(2)}, u32[]{:S(2)}) collective-permute-start(f32[16,128]{1,0:T(8,128)} %get-tuple-element.8), channel_id=1, source_target_pairs={{0,1},{1,0},{2,3},{3,2},{4,5},{5,4},{6,7},{7,6},{8,9},{9,8},{10,11... | collective-permute-start | bytes 24584 | tf_op jit(solution)/shard_map/ppermute | solution.py:370

commit v3 on v2

--- a/solution.py
+++ b/solution.py
@@ -13,7 +13,7 @@
 CODE_REACH = 3
 LOADING = 0.25
 BLOCK = 32
-STEP = 4
+STEP = 8
 LANES = 128
 HEAD = 8
 TILE = 96
@@ -42,37 +42,46 @@
 NT = ((1,), (1,))
 
 
-def eliminate(work, turned):
-    rows = lax.broadcasted_iota(jnp.int32, work.shape, 0)
-    scale = jnp.zeros_like(work)
+def eliminate(work):
+    count = BLOCK // 8
+    w = [work[8 * g : 8 * g + 8] for g in range(count)]
+    rows = lax.broadcasted_iota(jnp.int32, (8, LANES), 0)
+    even = lax.broadcasted_iota(jnp.int32, (8, LANES), 1) // BLOCK % 2 == 0
+    scale = [jnp.zeros((8, LANES), jnp.float32)] * count
+    spread = lambda x: jnp.broadcast_to(x, (8, LANES))
     for base in range(0, BLOCK, STEP):
-        col_re = [jnp.broadcast_to(work[:, base + t : base + t + 1], work.shape) for t in range(STEP)]
-        col_im = [
-            jnp.broadcast_to(work[:, BLOCK + base + t : BLOCK + base + t + 1], work.shape)
-            for t in range(STEP)
+        head = base // 8
+        live = range(head, count)
+        columns = lambda first: [
+            {g: spread(w[g][:, first + t : first + t + 1]) for g in live} for t in range(STEP)
         ]
+        col_re, col_im = columns(base), columns(BLOCK + base)
+        turned = jnp.where(
+            even, -pltpu.roll(w[head], LANES - BLOCK, 1), pltpu.roll(w[head], BLOCK, 1)
+        )
         for t in range(STEP):
-            j = base + t
-            pivot = jnp.broadcast_to(col_re[t][j : j + 1], (8, LANES))
-            inverse = jnp.concatenate([1.0 / pivot] * (BLOCK // 8), axis=0)
-            below = rows > j
-            m_re = jnp.where(below, col_re[t] * inverse, 0.0)
-            m_im = jnp.where(below, col_im[t] * inverse, 0.0)
+            r = (base + t) % 8
+            at = slice(r, r + 1)
+            inverse = 1.0 / spread(col_re[t][head][at])
+            scale[head] = jnp.where(rows == r, inverse, scale[head])
+            m_re = {g: col_re[t][g] * inverse for g in live}
+            m_im = {g: col_im[t][g] * inverse for g in live}
+            m_re[head] = jnp.where(rows > r, m_re[head], 0.0)
+            m_im[head] = jnp.where(rows > r, m_im[head], 0.0)
+            below = [g for g in live if g > head or r < 7]
             for u in range(t + 1, STEP):
-                e_re = jnp.broadcast_to(col_re[u][j : j + 1], work.shape)
-                e_im = jnp.broadcast_to(col_im[u][j : j + 1], work.shape)
-                col_re[u], col_im[u] = (
-                    col_re[u] - m_re * e_re + m_im * e_im,
-                    col_im[u] - m_re * e_im - m_im * e_re,
-                )
-            row = jnp.broadcast_to(work[j : j + 1], work.shape)
-            row_turned = jnp.broadcast_to(turned[j : j + 1], work.shape)
-            work, turned = (
-                work - m_re * row - m_im * row_turned,
-                turned - m_re * row_turned + m_im * row,
-            )
-            scale = jnp.where(rows == j, inverse, scale)
-    return work * jnp.sqrt(scale)
+                e_re, e_im = spread(col_re[u][head][at]), spread(col_im[u][head][at])
+                for g in below:
+                    col_re[u][g], col_im[u][g] = (
+                        col_re[u][g] - (m_re[g] * e_re - m_im[g] * e_im),
+                        col_im[u][g] - (m_re[g] * e_im + m_im[g] * e_re),
+                    )
+            row, row_turned = spread(w[head][at]), spread(turned[at])
+            if r < 7:
+                turned = turned - (m_re[head] * row_turned - m_im[head] * row)
+            for g in below:
+                w[g] = w[g] - (m_re[g] * row + m_im[g] * row_turned)
+    return jnp.concatenate(w, axis=0) * jnp.sqrt(jnp.concatenate(scale, axis=0))
 
 
 def split3(x):
@@ -217,8 +226,7 @@
                     [ref[:seen] for ref in (v_high, v_mid, v_low)],
                 )
         work = jnp.concatenate([d_re, d_im, unit, blank], axis=1)
-        turned = jnp.concatenate([-d_im, d_re, blank, unit], axis=1)
-        work = eliminate(work, turned)
+        work = eliminate(work)
         solved = dot6(split3(work[:, 2 * BLOCK :]), panel)
         mat[at:nxt, 2 * elements :] = solved[:, 2 * elements :]
         if k + 1 < steps:
@@ -245,8 +253,12 @@
     response = jnp.sum(jnp.where(own_lane, real, 0.0), axis=1, keepdims=True)
     factor = lax.rsqrt(jnp.where(response > 0.0, response, 1.0))
     both = jnp.concatenate([real * factor, imag * factor], axis=0)
-    own_ref[...] = pltpu.roll(both, LANES - 8, 1)
-    other_ref[...] = pltpu.roll(both, LANES - 8 - gate_dev, 1)
+    for ref, shift in ((own_ref, 8), (other_ref, 8 + gate_dev)):
+        moved = pltpu.roll(both, LANES - shift, 1)
+        for part in range(2):
+            rows = moved[8 * part : 8 * part + 8]
+            for b in range(2):
+                ref[part, b] = jnp.where(place_ref[0] == b, rows, 0.0)
 
 
 def adapt(place, code, chunks, steer_re, steer_im):
@@ -267,7 +279,7 @@
                 whole((8, elements)),
                 whole((8, elements)),
             ],
-            out_specs=[whole((16, LANES)), whole((16, LANES))],
+            out_specs=[whole((2, 2, 8, LANES))] * 2,
             scratch_shapes=[
                 pltpu.VMEM((gates - TILE + LANES + HEAD, elements), f32),
                 pltpu.VMEM((gates - TILE + LANES + HEAD, elements), f32),
@@ -279,60 +291,79 @@
             + [pltpu.VMEM((2 * elements, width), bf16)] * 3
             + [pltpu.VMEM((elements, 2 * elements), bf16)] * 3,
         ),
-        out_shape=[jax.ShapeDtypeStruct((16, LANES), f32)] * 2,
+        out_shape=[jax.ShapeDtypeStruct((2, 2, 8, LANES), f32)] * 2,
         name="adapt",
     )(place, code, chunks, steer_re, steer_im)
 
 
-def channel_kernel(raw_ref, taps_ref, table_ref, out_ref, filtered):
-    step = pl.program_id(0)
-    elem_dev = pl.num_programs(0)
-    rows = out_ref.shape[1] // 2
-    gate_dev = rows // 8
-    weights = [taps_ref[t] for t in range(TAPS)]
-    for g in range(gate_dev):
-        at = g * 8 * TAPS
-        piece = raw_ref[at : at + 8 * TAPS].astype(jnp.float32)
-        total = piece[0:8] * weights[0]
-        for t in range(1, TAPS):
-            total = total + piece[8 * t : 8 * t + 8] * weights[t]
-        to = pl.multiple_of((g * elem_dev + step) * 8, 8)
-        filtered[pl.ds(to, 8)] = total.astype(jnp.bfloat16).astype(jnp.float32)
-
-    @pl.when(step == elem_dev - 1)
-    def _():
-        sums = []
-        for r in range(2):
-            rows_r = jnp.concatenate(
-                [filtered[pl.ds(2 * j + r, rows, stride=8)] for j in range(4)], axis=1
-            ).astype(jnp.bfloat16)
-            sums.append(mm(table_ref[...], rows_r, NT, None))
-        half = out_ref.shape[0]
-        re = sums[0][:half] + sums[1][half:]
-        im = sums[1][:half] - sums[0][half:]
-        out_ref[...] = jnp.concatenate([re, im], axis=1).astype(jnp.bfloat16)
-
-
-def channelize(raw_samples, filter_taps, bin_total):
+def channel_kernel(raw_ref, taps_ref, table_ref, out_ref, raw, filtered, arrived):
+    elem_dev = arrived.shape[0]
+    dests, bin_dev, lanes = out_ref.shape
+    rows = lanes // 2
+    gate_dev = rows // elem_dev
+    per = gate_dev * 8 * TAPS
+    copies = [
+        pltpu.make_async_copy(
+            raw_ref.at[pl.ds(e * per, per)], raw.at[pl.ds(e * per, per)], arrived.at[e]
+        )
+        for e in range(elem_dev)
+    ]
+    for copy in copies:
+        copy.start()
+    pair = lax.broadcasted_iota(jnp.int32, (8, LANES), 0) // 2
+    weights = []
+    for t in range(TAPS):
+        weight = jnp.zeros((8, LANES), jnp.float32)
+        for j in range(CHANNELS // LANES):
+            piece = taps_ref[t : t + 1, j * LANES : (j + 1) * LANES]
+            weight = jnp.where(pair == j, piece, weight)
+        weights.append(weight)
+    for e, copy in enumerate(copies):
+        copy.wait()
+        for g in range(gate_dev):
+            at = e * per + g * 8 * TAPS
+            piece = raw[at : at + 8 * TAPS].astype(jnp.float32)
+            total = piece[0:8] * weights[0]
+            for t in range(1, TAPS):
+                total = total + piece[8 * t : 8 * t + 8] * weights[t]
+            to = (g * elem_dev + e) * 8
+            filtered[to : to + 8] = total.astype(jnp.bfloat16).astype(jnp.float32)
+    sums = []
+    for r in range(2):
+        rows_r = jnp.concatenate(
+            [filtered[pl.ds(2 * j + r, rows, stride=8)] for j in range(CHANNELS // LANES)], axis=1
+        ).astype(jnp.bfloat16)
+        sums.append(mm(table_ref[...], rows_r, NT, None))
+    half = dests * bin_dev
+    re = sums[0][:half] + sums[1][half:]
+    im = sums[1][:half] - sums[0][half:]
+    spectra = jnp.concatenate([re, im], axis=1).astype(jnp.bfloat16)
+    for d in range(dests):
+        out_ref[d] = spectra[bin_dev * d : bin_dev * (d + 1)]
+
+
+def channelize(raw_samples, filter_taps, bin_dev, dop_count):
     elem_dev, gate_dev = raw_samples.shape[:2]
     tiles = CHANNELS // LANES
     flat = raw_samples.reshape(elem_dev, gate_dev, 2, TAPS * tiles, LANES)
     flat = jnp.transpose(flat, (0, 1, 3, 2, 4)).reshape(-1, LANES)
-    taps = jnp.repeat(filter_taps.reshape(TAPS, tiles, 1, LANES), 2, axis=2).reshape(TAPS, 8, LANES)
     rows = gate_dev * elem_dev
     return pl.pallas_call(
         channel_kernel,
-        grid=(elem_dev,),
         in_specs=[
-            pl.BlockSpec((gate_dev * TAPS * tiles * 2, LANES), lambda e: (e, 0)),
-            pl.BlockSpec((TAPS, 8, LANES), lambda e: (0, 0, 0)),
-            pl.BlockSpec((2 * bin_total, CHANNELS), lambda e: (0, 0)),
+            pl.BlockSpec(memory_space=pl.ANY),
+            pl.BlockSpec(memory_space=pltpu.VMEM),
+            pl.BlockSpec(memory_space=pltpu.VMEM),
         ],
-        out_specs=pl.BlockSpec((bin_total, 2 * rows), lambda e: (0, 0)),
-        out_shape=jax.ShapeDtypeStruct((bin_total, 2 * rows), jnp.bfloat16),
-        scratch_shapes=[pltpu.VMEM((rows * 8, LANES), jnp.float32)],
+        out_specs=pl.BlockSpec(memory_space=pltpu.VMEM),
+        out_shape=jax.ShapeDtypeStruct((dop_count, bin_dev, 2 * rows), jnp.bfloat16),
+        scratch_shapes=[
+            pltpu.VMEM(flat.shape, jnp.bfloat16),
+            pltpu.VMEM((rows * 8, LANES), jnp.float32),
+            pltpu.SemaphoreType.DMA((elem_dev,)),
+        ],
         name="channelize",
-    )(flat, taps, dft_rows(bin_total))
+    )(flat, filter_taps, dft_rows(dop_count * bin_dev))
 
 
 def steering_rows(steer_row, elements):
@@ -350,8 +381,7 @@
     bin_dev, beams = steer_index.shape
     dop_count, rng_count = lax.axis_size("dop"), lax.axis_size("rng")
     elements = elem_dev * dop_count
-    bin_total = bin_dev * dop_count
-    spectra = channelize(raw_samples, filter_taps, bin_total)
+    spectra = channelize(raw_samples, filter_taps, bin_dev, dop_count)
     turned = lax.all_to_all(spectra, "dop", split_axis=0, concat_axis=0, tiled=True)
     turned = turned.reshape(dop_count, bin_dev, 2 * gate_dev, elem_dev)
     turned = jnp.transpose(turned, (1, 2, 0, 3)).reshape(bin_dev, 2 * gate_dev, elements)
@@ -368,11 +398,7 @@
     steer_re, steer_im = steering_rows(steer_row, elements)
     own, other = adapt(place, range_code, chunks, steer_re, steer_im)
     swapped = lax.ppermute(other, "rng", [(i, i ^ 1) for i in range(rng_count)])
-    trim = lambda x: x.reshape(2, 8, LANES)[:, :beams, :gate_dev]
-    own, swapped = trim(own), trim(swapped)
-    low = jnp.where(core == 0, own, swapped)
-    high = jnp.where(core == 0, swapped, own)
-    return jnp.stack([low, high], axis=1)
+    return (own + swapped)[:, :, :beams, :gate_dev]
 
 
 def solution(mesh):

time: 79.7 us -> 72 us (0.903)
  Pallas kernels: 25.5 us -> 20.7 us
  local copies, waits for them, and re-layouts: 4.47 us -> 1.68 us
    pallas_call x1, Pallas kernels: 19.9 us -> 16.8 us  [adapt(): pl.pallas_call(adapt_kernel, grid_spec=pltpu.PrefetchScalarGridSpec(num_s...]
    pallas_call x1, Pallas kernels: 5.61 us -> 3.9 us  [channelize(): pl.pallas_call(channel_kernel, in_specs=[pl.BlockSpec(memory_space=pl.ANY...]
    all_to_all x2 -> x1, local copies, waits for them, and re-layouts: 1.62 us -> 0.18 us  [shards(): lax.all_to_all(spectra, 'dop', split_axis=0, concat_axis=0, tiled=True)]
    add x0 -> x1, other arithmetic: none -> 1.32 us  [shards(): return (own + swapped)[:, :, :beams, :gate_dev]]
    another operation x2 -> x0, other arithmetic: 1.31 us -> none  [shards(): return jnp.stack([low, high], axis=1)]
  transfers between devices with their start and end apart: 2 -> 2, of which waited for: 2 -> 2; matrix products, arithmetic and copies ran while one was open for 2% -> 3% of each run, Pallas kernels for 0% -> 0%
where the time goes in v3:
time: 72 us; the launch traced here: 71.7 us
  blocking collectives  23.4 us (32%)
  Pallas kernels  20.7 us (29%)
  starting transfers between devices  15.8 us (22%)
  waiting for transfers between devices  7.92 us (11%)
  other arithmetic  2.08 us (3%)
  local copies, waits for them, and re-layouts  1.68 us (2%)
    all_gather x1, blocking collectives, shards(): chunks = lax.all_gather(chunk, 'rng', axis=0, tiled=False)  23.4 us
    pallas_call x1, Pallas kernels, adapt(): pl.pallas_call(adapt_kernel, grid_spec=pltpu.PrefetchScalarGridSpec(num_s...  16.8 us
    all_to_all x1, starting transfers between devices, shards(): lax.all_to_all(spectra, 'dop', split_axis=0, concat_axis=0, tiled=True)  13.7 us
    all_to_all x1, waiting for transfers between devices, shards(): lax.all_to_all(spectra, 'dop', split_axis=0, concat_axis=0, tiled=True)  6.71 us
    pallas_call x1, Pallas kernels, channelize(): pl.pallas_call(channel_kernel, in_specs=[pl.BlockSpec(memory_space=pl.ANY...  3.9 us
    ppermute x1, starting transfers between devices, shards(): swapped = lax.ppermute(other, 'rng', [(i, i ^ 1) for i in range(rng_count)])  2.06 us
  transfers between devices with their start and end apart: 2, of which 2 were waited for; matrix products, arithmetic and copies ran while one was open for 3% of the time, Pallas kernels for 0%

profile of v3, /device:TPU:1, one launch (start us, length us, event | category | flops | bytes accessed | tf_op | source)
XLA Modules:
  0.0 71.7 jit_solution(17875545851588942565)
XLA Ops:
  0.0 0.0 copy-start
  0.0 0.0 copy-start.1
  0.0 3.9 %channelize.1 = bf16[32,2,384]{2,1,0:T(2,128)(2,1)} custom-call(bf16[12288,128]{1,0:T(8,128)(2,1)} %bitcast.18, f32[8,512]{1,0:T(8,128)} %taps_ref.1, bf16[128,512]{1,0:T(8,128)(2,1)} %constant.49.clone.table_ref), custom_call_target="tpu_custom_call" | custom-call | tf_op jit(solution)/shard_map/channelize/pallas_call | solution.py:351
  3.9 13.7 %all-to-all-start = ((bf16[32,2,384]{2,1,0:T(2,128)(2,1)}), bf16[32,2,384]{2,1,0:T(2,128)(2,1)S(1)}, u32[]{:S(2)}, u32[]{:S(2)}) async-start(bf16[32,2,384]{2,1,0:T(2,128)(2,1)} %channelize.1), calls=%async_computation | async-start | bytes 98304 | tf_op jit(solution)/shard_map/all_to_all | solution.py:385
  17.6 0.0 copy-done
  17.7 0.0 copy-done.1
  17.7 0.1 fusion.5
  17.8 0.6 pad.12.steer_re_ref
  18.4 0.6 pad.13.steer_im_ref
  19.0 0.6 pad_add_fusion.place_ref
  19.7 6.7 %all-to-all-done = bf16[32,2,384]{2,1,0:T(2,128)(2,1)S(1)} async-done(((bf16[32,2,384]{2,1,0:T(2,128)(2,1)}), bf16[32,2,384]{2,1,0:T(2,128)(2,1)S(1)}, u32[]{:S(2)}, u32[]{:S(2)}) %all-to-all-start) | async-done | bytes 49184 | tf_op jit(solution)/shard_map/all_to_all | solution.py:385
  26.4 0.2 copy.16
  26.6 0.2 copy.17
  26.8 0.1 copy.18
  26.9 23.4 %all-gather = bf16[32,56,256]{2,1,0:T(8,128)(2,1)} all-gather(bf16[2,56,256]{2,1,0:T(8,128)(2,1)S(1)} %fusion.1), channel_id=2, replica_groups=mesh['dop'=32,'rng'=16] {'rng'}, dimensions={0}, use_global_device_ids=true | all-gather | bytes 974848 | tf_op jit(solution)/shard_map/all_gather | solution.py:393
  50.3 16.8 %adapt.1 = (f32[2,2,8,128]{3,2,1,0:T(8,128)}, f32[2,2,8,128]{3,2,1,0:T(8,128)}) custom-call(s32[3]{0:T(128)} %pad_add_fusion.place_ref, f32[2,7]{1,0:T(2,128)} %code_ref.1, bf16[16,2,56,256]{3,2,1,0:T(8,128)(2,1)} %bitcast.17, f32[8,256]{1,0:T(8,128)} %pad.12.steer_re_ref, f32[8,256]{1,0:T(8,128)} %pad.13.steer_im_ref), custom_call_target="tpu_custom_call" | custom-call | tf_op jit(solution)/shard_map/adapt/pallas_call | solution.py:271
  67.1 2.1 %collective-permute-start = (f32[2,2,8,128]{3,2,1,0:T(8,128)}, f32[2,2,8,128]{3,2,1,0:T(8,128)S(1)}, u32[]{:S(2)}, u32[]{:S(2)}) collective-permute-start(f32[2,2,8,128]{3,2,1,0:T(8,128)} %get-tuple-element.8), channel_id=1, source_target_pairs={{0,1},{1,0},{2,3},{3,2},{4,5},{5,4},{6,7},{7,6},{8,9},{9,8},{10,11... | collective-permute-start | bytes 49160 | tf_op jit(solution)/shard_map/ppermute | solution.py:400
  69.1 1.2 %collective-permute-done = f32[2,2,8,128]{3,2,1,0:T(8,128)S(1)} collective-permute-done((f32[2,2,8,128]{3,2,1,0:T(8,128)}, f32[2,2,8,128]{3,2,1,0:T(8,128)S(1)}, u32[]{:S(2)}, u32[]{:S(2)}) %collective-permute-start) | collective-permute-done | bytes 16416 | tf_op jit(solution)/shard_map/ppermute | solution.py:400
  70.3 1.3 %slice_add_fusion = f32[2,2,4,24]{3,2,1,0:T(4,128)} fusion(f32[2,2,8,128]{3,2,1,0:T(8,128)S(1)} %collective-permute-done, f32[2,2,8,128]{3,2,1,0:T(8,128)} %get-tuple-element.7), kind=kLoop, calls=%fused_computation.3 | loop fusion | flops 384 | bytes 4608 | tf_op jit(solution)/shard_map/add | solution.py:401
  (4 shorter events, 0.0 us)
Async XLA Ops:
  0.0 17.6 %copy-start = (s32[2,24]{1,0:T(2,128)S(1)}, s32[2,24]{1,0:T(2,128)}, u32[]{:S(2)}) copy-start(s32[2,24]{1,0:T(2,128)} %param.9) | copy-start | bytes 580
  0.0 17.7 %copy-start.1 = (s32[2,4]{1,0:T(2,128)S(1)}, s32[2,4]{1,0:T(2,128)}, u32[]{:S(2)}) copy-start(s32[2,4]{1,0:T(2,128)} %param.10) | copy-start | bytes 100
  3.9 22.5 %all-to-all-start = ((bf16[32,2,384]{2,1,0:T(2,128)(2,1)}), bf16[32,2,384]{2,1,0:T(2,128)(2,1)S(1)}, u32[]{:S(2)}, u32[]{:S(2)}) async-start(bf16[32,2,384]{2,1,0:T(2,128)(2,1)} %channelize.1), calls=%async_computation | async-start | bytes 98304 | tf_op jit(solution)/shard_map/all_to_all | solution.py:385
  67.1 3.3 %collective-permute-start = (f32[2,2,8,128]{3,2,1,0:T(8,128)}, f32[2,2,8,128]{3,2,1,0:T(8,128)S(1)}, u32[]{:S(2)}, u32[]{:S(2)}) collective-permute-start(f32[2,2,8,128]{3,2,1,0:T(8,128)} %get-tuple-element.8), channel_id=1, source_target_pairs={{0,1},{1,0},{2,3},{3,2},{4,5},{5,4},{6,7},{7,6},{8,9},{9,8},{10,11... | collective-permute-start | bytes 49160 | tf_op jit(solution)/shard_map/ppermute | solution.py:400

commit v4 on v3

--- a/solution.py
+++ b/solution.py
@@ -52,17 +52,27 @@
     for base in range(0, BLOCK, STEP):
         head = base // 8
         live = range(head, count)
-        columns = lambda first: [
-            {g: spread(w[g][:, first + t : first + t + 1]) for g in live} for t in range(STEP)
-        ]
-        col_re, col_im = columns(base), columns(BLOCK + base)
+        col_re = [{} for _ in range(STEP)]
+        col_im = [{} for _ in range(STEP)]
+        for g in live:
+            for t in range(STEP):
+                c = 2 * BLOCK + base + t
+                col_re[t][g] = spread(w[g][:, c : c + 1])
+                col_im[t][g] = spread(w[g][:, BLOCK + c : BLOCK + c + 1])
         turned = jnp.where(
             even, -pltpu.roll(w[head], LANES - BLOCK, 1), pltpu.roll(w[head], BLOCK, 1)
         )
         for t in range(STEP):
             r = (base + t) % 8
             at = slice(r, r + 1)
-            inverse = 1.0 / spread(col_re[t][head][at])
+            if t % 2 == 0:
+                nxt = slice(r + 1, r + 2)
+                first, second = spread(col_re[t][head][at]), spread(col_re[t + 1][head][nxt])
+                x_re, x_im = spread(col_re[t + 1][head][at]), spread(col_im[t + 1][head][at])
+                inverse = 1.0 / first
+                following = first * (1.0 / (first * second - (x_re * x_re + x_im * x_im)))
+            else:
+                inverse = following
             scale[head] = jnp.where(rows == r, inverse, scale[head])
             m_re = {g: col_re[t][g] * inverse for g in live}
             m_im = {g: col_im[t][g] * inverse for g in live}
@@ -136,6 +146,7 @@
     s_low,
 ):
     chunk_count, _, _, elements = chunks_ref.shape
+    _, bin_dev, beams, _ = own_ref.shape
     gate_dev = (chunks_ref.shape[2] - MASK_ROWS) // 2
     gates = chunk_count * gate_dev
     f32, bf16 = jnp.float32, jnp.bfloat16
@@ -225,9 +236,9 @@
                     [ref[nxt : nxt + BLOCK, :seen] for ref in (s_high, s_mid, s_low)],
                     [ref[:seen] for ref in (v_high, v_mid, v_low)],
                 )
-        work = jnp.concatenate([d_re, d_im, unit, blank], axis=1)
+        work = jnp.concatenate([unit, blank, d_re, d_im], axis=1)
         work = eliminate(work)
-        solved = dot6(split3(work[:, 2 * BLOCK :]), panel)
+        solved = dot6(split3(work[:, : 2 * BLOCK]), panel)
         mat[at:nxt, 2 * elements :] = solved[:, 2 * elements :]
         if k + 1 < steps:
             trail = stack_turned(solved, elements, -1)
@@ -256,16 +267,17 @@
     for ref, shift in ((own_ref, 8), (other_ref, 8 + gate_dev)):
         moved = pltpu.roll(both, LANES - shift, 1)
         for part in range(2):
-            rows = moved[8 * part : 8 * part + 8]
-            for b in range(2):
+            rows = moved[8 * part : 8 * part + beams, :gate_dev]
+            for b in range(bin_dev):
                 ref[part, b] = jnp.where(place_ref[0] == b, rows, 0.0)
 
 
-def adapt(place, code, chunks, steer_re, steer_im):
-    count, _, rows, elements = chunks.shape
+def adapt(place, code, chunks, steer_re, steer_im, beams):
+    count, bin_dev, rows, elements = chunks.shape
     gate_dev = (rows - MASK_ROWS) // 2
     gates = count * gate_dev
     width = 2 * elements + LANES
+    out = (2, bin_dev, beams, gate_dev)
     whole = lambda shape: pl.BlockSpec(shape, lambda i, p: (0,) * len(shape))
     f32, bf16 = jnp.float32, jnp.bfloat16
     return pl.pallas_call(
@@ -279,7 +291,7 @@
                 whole((8, elements)),
                 whole((8, elements)),
             ],
-            out_specs=[whole((2, 2, 8, LANES))] * 2,
+            out_specs=[whole(out)] * 2,
             scratch_shapes=[
                 pltpu.VMEM((gates - TILE + LANES + HEAD, elements), f32),
                 pltpu.VMEM((gates - TILE + LANES + HEAD, elements), f32),
@@ -291,7 +303,7 @@
             + [pltpu.VMEM((2 * elements, width), bf16)] * 3
             + [pltpu.VMEM((elements, 2 * elements), bf16)] * 3,
         ),
-        out_shape=[jax.ShapeDtypeStruct((2, 2, 8, LANES), f32)] * 2,
+        out_shape=[jax.ShapeDtypeStruct(out, f32)] * 2,
         name="adapt",
     )(place, code, chunks, steer_re, steer_im)
 
@@ -396,9 +408,9 @@
     place = jnp.stack([core, position, position ^ 1]).astype(jnp.int32)
     steer_row = lax.dynamic_index_in_dim(steer_index, core, 0, keepdims=False)
     steer_re, steer_im = steering_rows(steer_row, elements)
-    own, other = adapt(place, range_code, chunks, steer_re, steer_im)
+    own, other = adapt(place, range_code, chunks, steer_re, steer_im, beams)
     swapped = lax.ppermute(other, "rng", [(i, i ^ 1) for i in range(rng_count)])
-    return (own + swapped)[:, :, :beams, :gate_dev]
+    return own + swapped
 
 
 def solution(mesh):

time: 72 us -> 70.4 us (0.978)
  Pallas kernels: 20.7 us -> 19.2 us
    pallas_call x1, Pallas kernels: 16.8 us -> 15.3 us  [adapt(): pl.pallas_call(adapt_kernel, grid_spec=pltpu.PrefetchScalarGridSpec(num_s...]
where the time goes in v4:
time: 70.4 us; the launch traced here: 70.1 us
  blocking collectives  23.4 us (33%)
  Pallas kernels  19.2 us (27%)
  starting transfers between devices  15.8 us (22%)
  waiting for transfers between devices  7.91 us (11%)
  other arithmetic  2.06 us (3%)
  local copies, waits for them, and re-layouts  1.68 us (2%)
    all_gather x1, blocking collectives, shards(): chunks = lax.all_gather(chunk, 'rng', axis=0, tiled=False)  23.4 us
    pallas_call x1, Pallas kernels, adapt(): pl.pallas_call(adapt_kernel, grid_spec=pltpu.PrefetchScalarGridSpec(num_s...  15.3 us
    all_to_all x1, starting transfers between devices, shards(): lax.all_to_all(spectra, 'dop', split_axis=0, concat_axis=0, tiled=True)  13.7 us
    all_to_all x1, waiting for transfers between devices, shards(): lax.all_to_all(spectra, 'dop', split_axis=0, concat_axis=0, tiled=True)  6.71 us
    pallas_call x1, Pallas kernels, channelize(): pl.pallas_call(channel_kernel, in_specs=[pl.BlockSpec(memory_space=pl.ANY...  3.9 us
    ppermute x1, starting transfers between devices, shards(): swapped = lax.ppermute(other, 'rng', [(i, i ^ 1) for i in range(rng_count)])  2.06 us
  transfers between devices with their start and end apart: 2, of which 2 were waited for; matrix products, arithmetic and copies ran while one was open for 3% of the time, Pallas kernels for 0%

profile of v4, /device:TPU:1, one launch (start us, length us, event | category | flops | bytes accessed | tf_op | source)
XLA Modules:
  0.0 70.1 jit_solution(1970957440448722792)
XLA Ops:
  0.0 0.0 copy-start
  0.0 0.0 copy-start.1
  0.0 3.9 %channelize.1 = bf16[32,2,384]{2,1,0:T(2,128)(2,1)} custom-call(bf16[12288,128]{1,0:T(8,128)(2,1)} %bitcast.18, f32[8,512]{1,0:T(8,128)} %taps_ref.1, bf16[128,512]{1,0:T(8,128)(2,1)} %constant.49.clone.table_ref), custom_call_target="tpu_custom_call" | custom-call | tf_op jit(solution)/shard_map/channelize/pallas_call | solution.py:363
  3.9 13.7 %all-to-all-start = ((bf16[32,2,384]{2,1,0:T(2,128)(2,1)}), bf16[32,2,384]{2,1,0:T(2,128)(2,1)S(1)}, u32[]{:S(2)}, u32[]{:S(2)}) async-start(bf16[32,2,384]{2,1,0:T(2,128)(2,1)} %channelize.1), calls=%async_computation | async-start | bytes 98304 | tf_op jit(solution)/shard_map/all_to_all | solution.py:397
  17.6 0.0 copy-done
  17.7 0.0 copy-done.1
  17.7 0.1 fusion.5
  17.8 0.6 pad.12.steer_re_ref
  18.4 0.6 pad.13.steer_im_ref
  19.0 0.6 pad_add_fusion.place_ref
  19.7 6.7 %all-to-all-done = bf16[32,2,384]{2,1,0:T(2,128)(2,1)S(1)} async-done(((bf16[32,2,384]{2,1,0:T(2,128)(2,1)}), bf16[32,2,384]{2,1,0:T(2,128)(2,1)S(1)}, u32[]{:S(2)}, u32[]{:S(2)}) %all-to-all-start) | async-done | bytes 49184 | tf_op jit(solution)/shard_map/all_to_all | solution.py:397
  26.4 0.2 copy.16
  26.6 0.2 copy.17
  26.8 0.1 copy.18
  26.9 23.4 %all-gather = bf16[32,56,256]{2,1,0:T(8,128)(2,1)} all-gather(bf16[2,56,256]{2,1,0:T(8,128)(2,1)S(1)} %fusion.1), channel_id=2, replica_groups=mesh['dop'=32,'rng'=16] {'rng'}, dimensions={0}, use_global_device_ids=true | all-gather | bytes 974848 | tf_op jit(solution)/shard_map/all_gather | solution.py:405
  50.3 15.3 %adapt.1 = (f32[2,2,4,24]{3,2,1,0:T(4,128)}, f32[2,2,4,24]{3,2,1,0:T(4,128)}) custom-call(s32[3]{0:T(128)} %pad_add_fusion.place_ref, f32[2,7]{1,0:T(2,128)} %code_ref.1, bf16[16,2,56,256]{3,2,1,0:T(8,128)(2,1)} %bitcast.17, f32[8,256]{1,0:T(8,128)} %pad.12.steer_re_ref, f32[8,256]{1,0:T(8,128)} %pad.13.steer_im_ref), custom_call_target="tpu_custom_call" | custom-call | tf_op jit(solution)/shard_map/adapt/pallas_call | solution.py:283
  65.6 2.1 %collective-permute-start = (f32[2,2,4,24]{3,2,1,0:T(4,128)}, f32[2,2,4,24]{3,2,1,0:T(4,128)S(1)}, u32[]{:S(2)}, u32[]{:S(2)}) collective-permute-start(f32[2,2,4,24]{3,2,1,0:T(4,128)} %get-tuple-element.8), channel_id=1, source_target_pairs={{0,1},{1,0},{2,3},{3,2},{4,5},{5,4},{6,7},{7,6},{8,9},{9,8},{10,11... | collective-permute-start | bytes 4616 | tf_op jit(solution)/shard_map/ppermute | solution.py:412
  67.6 1.2 %collective-permute-done = f32[2,2,4,24]{3,2,1,0:T(4,128)S(1)} collective-permute-done((f32[2,2,4,24]{3,2,1,0:T(4,128)}, f32[2,2,4,24]{3,2,1,0:T(4,128)S(1)}, u32[]{:S(2)}, u32[]{:S(2)}) %collective-permute-start) | collective-permute-done | bytes 1568 | tf_op jit(solution)/shard_map/ppermute | solution.py:412
  68.8 1.3 %add.33 = f32[2,2,4,24]{3,2,1,0:T(4,128)} add(f32[2,2,4,24]{3,2,1,0:T(4,128)} %get-tuple-element.7, f32[2,2,4,24]{3,2,1,0:T(4,128)S(1)} %collective-permute-done) | non-fusion elementwise | flops 384 | bytes 4608 | tf_op jit(solution)/shard_map/add | solution.py:413
  (4 shorter events, 0.0 us)
Async XLA Ops:
  0.0 17.6 %copy-start = (s32[2,24]{1,0:T(2,128)S(1)}, s32[2,24]{1,0:T(2,128)}, u32[]{:S(2)}) copy-start(s32[2,24]{1,0:T(2,128)} %param.9) | copy-start | bytes 580
  0.0 17.7 %copy-start.1 = (s32[2,4]{1,0:T(2,128)S(1)}, s32[2,4]{1,0:T(2,128)}, u32[]{:S(2)}) copy-start(s32[2,4]{1,0:T(2,128)} %param.10) | copy-start | bytes 100
  3.9 22.5 %all-to-all-start = ((bf16[32,2,384]{2,1,0:T(2,128)(2,1)}), bf16[32,2,384]{2,1,0:T(2,128)(2,1)S(1)}, u32[]{:S(2)}, u32[]{:S(2)}) async-start(bf16[32,2,384]{2,1,0:T(2,128)(2,1)} %channelize.1), calls=%async_computation | async-start | bytes 98304 | tf_op jit(solution)/shard_map/all_to_all | solution.py:397
  65.6 3.3 %collective-permute-start = (f32[2,2,4,24]{3,2,1,0:T(4,128)}, f32[2,2,4,24]{3,2,1,0:T(4,128)S(1)}, u32[]{:S(2)}, u32[]{:S(2)}) collective-permute-start(f32[2,2,4,24]{3,2,1,0:T(4,128)} %get-tuple-element.8), channel_id=1, source_target_pairs={{0,1},{1,0},{2,3},{3,2},{4,5},{5,4},{6,7},{7,6},{8,9},{9,8},{10,11... | collective-permute-start | bytes 4616 | tf_op jit(solution)/shard_map/ppermute | solution.py:412

commit v5 on v4

--- a/solution.py
+++ b/solution.py
@@ -112,13 +112,13 @@
     return first[:count] + (first[count : 2 * count] + second[:count] + small)
 
 
-def stack_turned(x, elements, sign):
+def stack_turned(x, half, sign):
     lane = lax.broadcasted_iota(jnp.int32, (x.shape[0], LANES), 1)
-    tail = pltpu.roll(x[:, 2 * elements :], 64, 1)
+    tail = pltpu.roll(x[:, 2 * half :], 64, 1)
     tail = jnp.where((lane < 64) == (sign > 0), -tail, tail)
     out = []
     for whole, end in zip(split3(x), split3(tail)):
-        real, imag = whole[:, :elements], whole[:, elements : 2 * elements]
+        real, imag = whole[:, :half], whole[:, half : 2 * half]
         real, imag = (-imag, real) if sign > 0 else (imag, -real)
         out.append(jnp.concatenate([whole, jnp.concatenate([real, imag, end], axis=1)], axis=0))
     return out
@@ -158,7 +158,7 @@
     )
     masks = []
     for c in range(chunk_count):
-        chunk = chunks_ref[c, 0].astype(f32)
+        chunk = chunks_ref[c, place_ref[0]].astype(f32)
         at = HEAD + c * gate_dev
         sig_re[at : at + gate_dev] = chunk[:gate_dev]
         sig_im[at : at + gate_dev] = chunk[gate_dev : 2 * gate_dev]
@@ -222,34 +222,49 @@
     unit = jnp.where(lax.broadcasted_iota(jnp.int32, (BLOCK, BLOCK), 0) == lane, 1.0, 0.0)
     blank = jnp.zeros((BLOCK, BLOCK), f32)
     steps = elements // BLOCK
+    start = lambda k: k * BLOCK // LANES * LANES
+    pick = lambda ref, rows, lo: jnp.concatenate(
+        [ref[rows, lo:elements], ref[rows, elements + lo : 2 * elements], ref[rows, 2 * elements :]],
+        axis=1,
+    )
     acc = mat[0:BLOCK]
     for k in range(steps):
         at, nxt = k * BLOCK, (k + 1) * BLOCK
         seen = 2 * at
-        d_re = acc[:, at:nxt]
-        d_im = acc[:, elements + at : elements + nxt]
-        panel = stack_turned(acc, elements, 1)
+        first, following = start(k), start(k + 1)
+        half = elements - first
+        here = at - first
+        d_re = acc[:, here : here + BLOCK]
+        d_im = acc[:, half + here : half + here + BLOCK]
+        panel = stack_turned(acc, half, 1)
         if k + 1 < steps:
-            later = mat[nxt : nxt + BLOCK]
+            later = pick(mat, slice(nxt, nxt + BLOCK), following)
             if k > 0:
                 later = later - dot6(
                     [ref[nxt : nxt + BLOCK, :seen] for ref in (s_high, s_mid, s_low)],
-                    [ref[:seen] for ref in (v_high, v_mid, v_low)],
+                    [pick(ref, slice(0, seen), following) for ref in (v_high, v_mid, v_low)],
                 )
         work = jnp.concatenate([unit, blank, d_re, d_im], axis=1)
         work = eliminate(work)
         solved = dot6(split3(work[:, : 2 * BLOCK]), panel)
-        mat[at:nxt, 2 * elements :] = solved[:, 2 * elements :]
+        mat[at:nxt, 2 * elements :] = solved[:, 2 * half :]
         if k + 1 < steps:
-            trail = stack_turned(solved, elements, -1)
-            first = nxt // LANES * LANES
-            stem = jnp.concatenate(
-                [solved[:, first:elements], solved[:, elements + first : 2 * elements]], axis=0
-            ).T
-            stems = split3(stem[nxt - first :])
+            drop = following - first
+            if drop:
+                solved = jnp.concatenate(
+                    [solved[:, drop:half], solved[:, half + drop : 2 * half], solved[:, 2 * half :]],
+                    axis=1,
+                )
+            half = elements - following
+            trail = stack_turned(solved, half, -1)
+            stem = jnp.concatenate([solved[:, :half], solved[:, half : 2 * half]], axis=0).T
+            stems = split3(stem[nxt - following :])
             acc = later - dot6([part[:BLOCK] for part in stems], trail)
             for ref, part in zip((v_high, v_mid, v_low), trail):
-                ref[seen : seen + 2 * BLOCK] = part
+                rows = slice(seen, seen + 2 * BLOCK)
+                ref[rows, following:elements] = part[:, :half]
+                ref[rows, elements + following : 2 * elements] = part[:, half : 2 * half]
+                ref[rows, 2 * elements :] = part[:, 2 * half :]
             for ref, part in zip((s_high, s_mid, s_low), stems):
                 ref[nxt:, seen : seen + 2 * BLOCK] = part
 
@@ -278,7 +293,6 @@
     gates = count * gate_dev
     width = 2 * elements + LANES
     out = (2, bin_dev, beams, gate_dev)
-    whole = lambda shape: pl.BlockSpec(shape, lambda i, p: (0,) * len(shape))
     f32, bf16 = jnp.float32, jnp.bfloat16
     return pl.pallas_call(
         adapt_kernel,
@@ -287,11 +301,11 @@
             grid=(1,),
             in_specs=[
                 pl.BlockSpec(memory_space=pltpu.SMEM),
-                pl.BlockSpec((count, 1, rows, elements), lambda i, p: (0, p[0], 0, 0)),
-                whole((8, elements)),
-                whole((8, elements)),
+                pl.BlockSpec(memory_space=pltpu.VMEM),
+                pl.BlockSpec(memory_space=pltpu.VMEM),
+                pl.BlockSpec(memory_space=pltpu.VMEM),
             ],
-            out_specs=[whole(out)] * 2,
+            out_specs=[pl.BlockSpec(memory_space=pltpu.VMEM)] * 2,
             scratch_shapes=[
                 pltpu.VMEM((gates - TILE + LANES + HEAD, elements), f32),
                 pltpu.VMEM((gates - TILE + LANES + HEAD, elements), f32),
@@ -303,13 +317,18 @@
             + [pltpu.VMEM((2 * elements, width), bf16)] * 3
             + [pltpu.VMEM((elements, 2 * elements), bf16)] * 3,
         ),
-        out_shape=[jax.ShapeDtypeStruct(out, f32)] * 2,
+        out_shape=[pltpu.VMEM(out, f32)] * 2,
         name="adapt",
     )(place, code, chunks, steer_re, steer_im)
 
 
-def channel_kernel(raw_ref, taps_ref, table_ref, out_ref, raw, filtered, arrived):
+def channel_kernel(
+    raw_ref, taps_hbm, table_hbm, out_ref, raw, filtered, taps_ref, table_ref, arrived, small
+):
     elem_dev = arrived.shape[0]
+    get_taps = pltpu.make_async_copy(taps_hbm, taps_ref, small.at[0])
+    get_table = pltpu.make_async_copy(table_hbm, table_ref, small.at[1])
+    get_taps.start()
     dests, bin_dev, lanes = out_ref.shape
     rows = lanes // 2
     gate_dev = rows // elem_dev
@@ -322,6 +341,8 @@
     ]
     for copy in copies:
         copy.start()
+    get_table.start()
+    get_taps.wait()
     pair = lax.broadcasted_iota(jnp.int32, (8, LANES), 0) // 2
     weights = []
     for t in range(TAPS):
@@ -340,6 +361,7 @@
                 total = total + piece[8 * t : 8 * t + 8] * weights[t]
             to = (g * elem_dev + e) * 8
             filtered[to : to + 8] = total.astype(jnp.bfloat16).astype(jnp.float32)
+    get_table.wait()
     sums = []
     for r in range(2):
         rows_r = jnp.concatenate(
@@ -360,22 +382,22 @@
     flat = raw_samples.reshape(elem_dev, gate_dev, 2, TAPS * tiles, LANES)
     flat = jnp.transpose(flat, (0, 1, 3, 2, 4)).reshape(-1, LANES)
     rows = gate_dev * elem_dev
+    table = dft_rows(dop_count * bin_dev)
     return pl.pallas_call(
         channel_kernel,
-        in_specs=[
-            pl.BlockSpec(memory_space=pl.ANY),
-            pl.BlockSpec(memory_space=pltpu.VMEM),
-            pl.BlockSpec(memory_space=pltpu.VMEM),
-        ],
+        in_specs=[pl.BlockSpec(memory_space=pl.ANY)] * 3,
         out_specs=pl.BlockSpec(memory_space=pltpu.VMEM),
-        out_shape=jax.ShapeDtypeStruct((dop_count, bin_dev, 2 * rows), jnp.bfloat16),
+        out_shape=pltpu.VMEM((dop_count, bin_dev, 2 * rows), jnp.bfloat16),
         scratch_shapes=[
             pltpu.VMEM(flat.shape, jnp.bfloat16),
             pltpu.VMEM((rows * 8, LANES), jnp.float32),
+            pltpu.VMEM(filter_taps.shape, jnp.float32),
+            pltpu.VMEM(table.shape, jnp.bfloat16),
             pltpu.SemaphoreType.DMA((elem_dev,)),
+            pltpu.SemaphoreType.DMA((2,)),
         ],
         name="channelize",
-    )(flat, filter_taps, dft_rows(dop_count * bin_dev))
+    )(flat, filter_taps, table)
 
 
 def steering_rows(steer_row, elements):
@@ -408,6 +430,9 @@
     place = jnp.stack([core, position, position ^ 1]).astype(jnp.int32)
     steer_row = lax.dynamic_index_in_dim(steer_index, core, 0, keepdims=False)
     steer_re, steer_im = steering_rows(steer_row, elements)
+    chunks, steer_re, steer_im = (
+        pltpu.with_memory_space_constraint(x, pltpu.VMEM) for x in (chunks, steer_re, steer_im)
+    )
     own, other = adapt(place, range_code, chunks, steer_re, steer_im, beams)
     swapped = lax.ppermute(other, "rng", [(i, i ^ 1) for i in range(rng_count)])
     return own + swapped

time: 70.4 us -> 66.2 us (0.940)
  Pallas kernels: 19.2 us -> 17.3 us
  blocking collectives: 23.4 us -> 22 us
  local copies, waits for them, and re-layouts: 1.68 us -> 0.49 us
  waiting for transfers between devices: 7.91 us -> 8.86 us
    all_gather x1, blocking collectives: 23.4 us -> 22 us  [shards(): chunks = lax.all_gather(chunk, 'rng', axis=0, tiled=False)]
    pallas_call x1, Pallas kernels: 15.3 us -> 14.1 us  [adapt(): pl.pallas_call(adapt_kernel, grid_spec=pltpu.PrefetchScalarGridSpec(num_s...]
    pad x2, local copies, waits for them, and re-layouts: 1.2 us -> 0.01 us  [steering_rows(): return (jnp.pad(jnp.cos(phases), pad), jnp.pad(jnp.sin(phases), pad))]
    all_to_all x1, waiting for transfers between devices: 6.71 us -> 7.86 us  [shards(): lax.all_to_all(spectra, 'dop', split_axis=0, concat_axis=0, tiled=True)]
  transfers between devices with their start and end apart: 2 -> 2, of which waited for: 2 -> 2; matrix products, arithmetic and copies ran while one was open for 3% -> 1% of each run, Pallas kernels for 0% -> 0%
where the time goes in v5:
time: 66.2 us; the launch traced here: 66 us
  blocking collectives  22 us (33%)
  Pallas kernels  17.3 us (26%)
  starting transfers between devices  15.8 us (24%)
  waiting for transfers between devices  8.86 us (13%)
  other arithmetic  1.39 us (2%)
    all_gather x1, blocking collectives, shards(): chunks = lax.all_gather(chunk, 'rng', axis=0, tiled=False)  22 us
    pallas_call x1, Pallas kernels, adapt(): pl.pallas_call(adapt_kernel, grid_spec=pltpu.PrefetchScalarGridSpec(num_s...  14.1 us
    all_to_all x1, starting transfers between devices, shards(): lax.all_to_all(spectra, 'dop', split_axis=0, concat_axis=0, tiled=True)  13.7 us
    all_to_all x1, waiting for transfers between devices, shards(): lax.all_to_all(spectra, 'dop', split_axis=0, concat_axis=0, tiled=True)  7.86 us
    pallas_call x1, Pallas kernels, channelize(): pl.pallas_call(channel_kernel, in_specs=[pl.BlockSpec(memory_space=pl.ANY...  3.25 us
    ppermute x1, starting transfers between devices, shards(): swapped = lax.ppermute(other, 'rng', [(i, i ^ 1) for i in range(rng_count)])  2.06 us
  transfers between devices with their start and end apart: 2, of which 2 were waited for; matrix products, arithmetic and copies ran while one was open for 1% of the time, Pallas kernels for 0%

profile of v5, /device:TPU:1, one launch (start us, length us, event | category | flops | bytes accessed | tf_op | source)
XLA Modules:
  0.0 66.0 jit_solution(9428114661874376043)
XLA Ops:
  0.0 0.0 copy-start
  0.0 0.0 copy-start.1
  0.0 3.3 %channelize.1 = bf16[32,2,384]{2,1,0:T(2,128)(2,1)} custom-call(bf16[12288,128]{1,0:T(8,128)(2,1)} %bitcast.18, f32[8,512]{1,0:T(8,128)} %taps_hbm.1, bf16[128,512]{1,0:T(8,128)(2,1)} %constant.49.clone.table_hbm), custom_call_target="tpu_custom_call" | custom-call | tf_op jit(solution)/shard_map/channelize/pallas_call | solution.py:386
  3.3 13.7 %all-to-all-start = ((bf16[32,2,384]{2,1,0:T(2,128)(2,1)}), bf16[32,2,384]{2,1,0:T(2,128)(2,1)S(1)}, u32[]{:S(2)}, u32[]{:S(2)}) async-start(bf16[32,2,384]{2,1,0:T(2,128)(2,1)} %channelize.1), calls=%async_computation | async-start | bytes 98304 | tf_op jit(solution)/shard_map/all_to_all | solution.py:419
  17.0 0.0 copy-done
  17.0 0.0 copy-done.1
  17.1 0.1 fusion.5
  17.2 0.6 pad_add_fusion.place_ref
  17.9 7.9 %all-to-all-done = bf16[32,2,384]{2,1,0:T(2,128)(2,1)S(1)} async-done(((bf16[32,2,384]{2,1,0:T(2,128)(2,1)}), bf16[32,2,384]{2,1,0:T(2,128)(2,1)S(1)}, u32[]{:S(2)}, u32[]{:S(2)}) %all-to-all-start) | async-done | bytes 49184 | tf_op jit(solution)/shard_map/all_to_all | solution.py:419
  25.7 0.2 copy.16
  25.9 0.2 copy.17
  26.1 0.1 copy.18
  26.2 22.0 %all-gather = bf16[32,56,256]{2,1,0:T(8,128)(2,1)S(1)} all-gather(bf16[2,56,256]{2,1,0:T(8,128)(2,1)S(1)} %fusion.1), channel_id=2, replica_groups=mesh['dop'=32,'rng'=16] {'rng'}, dimensions={0}, use_global_device_ids=true | all-gather | bytes 974848 | tf_op jit(solution)/shard_map/all_gather | solution.py:427
  48.2 14.1 %adapt.1 = (f32[2,2,4,24]{3,2,1,0:T(4,128)S(1)}, f32[2,2,4,24]{3,2,1,0:T(4,128)S(1)}) custom-call(s32[3]{0:T(128)} %pad_add_fusion.place_ref, f32[2,7]{1,0:T(2,128)} %code_ref.1, bf16[16,2,56,256]{3,2,1,0:T(8,128)(2,1)S(1)} %bitcast.17, f32[8,256]{1,0:T(8,128)S(1)} %pad.12.steer_re_ref, f32[8,256]{1,0:T(8,128)S(1)} %pad.13.steer_im_ref), custom_call_target="tpu_custom_call" | custom-call | tf_op jit(solution)/shard_map/adapt/pallas_call | solution.py:297
  62.3 2.1 %collective-permute-start = (f32[2,2,4,24]{3,2,1,0:T(4,128)S(1)}, f32[2,2,4,24]{3,2,1,0:T(4,128)S(1)}, u32[]{:S(2)}, u32[]{:S(2)}) collective-permute-start(f32[2,2,4,24]{3,2,1,0:T(4,128)S(1)} %get-tuple-element.8), channel_id=1, source_target_pairs={{0,1},{1,0},{2,3},{3,2},{4,5},{5,4},{6,7},{7,6},{8,9},{9,8},{10,11... | collective-permute-start | bytes 4616 | tf_op jit(solution)/shard_map/ppermute | solution.py:437
  64.4 1.0 %collective-permute-done = f32[2,2,4,24]{3,2,1,0:T(4,128)S(1)} collective-permute-done((f32[2,2,4,24]{3,2,1,0:T(4,128)S(1)}, f32[2,2,4,24]{3,2,1,0:T(4,128)S(1)}, u32[]{:S(2)}, u32[]{:S(2)}) %collective-permute-start) | collective-permute-done | bytes 1568 | tf_op jit(solution)/shard_map/ppermute | solution.py:437
  65.4 0.6 add.33
  (6 shorter events, 0.0 us)
Async XLA Ops:
  0.0 17.0 %copy-start = (s32[2,24]{1,0:T(2,128)S(1)}, s32[2,24]{1,0:T(2,128)}, u32[]{:S(2)}) copy-start(s32[2,24]{1,0:T(2,128)} %param.9) | copy-start | bytes 580
  0.0 17.0 %copy-start.1 = (s32[2,4]{1,0:T(2,128)S(1)}, s32[2,4]{1,0:T(2,128)}, u32[]{:S(2)}) copy-start(s32[2,4]{1,0:T(2,128)} %param.10) | copy-start | bytes 100
  3.3 22.5 %all-to-all-start = ((bf16[32,2,384]{2,1,0:T(2,128)(2,1)}), bf16[32,2,384]{2,1,0:T(2,128)(2,1)S(1)}, u32[]{:S(2)}, u32[]{:S(2)}) async-start(bf16[32,2,384]{2,1,0:T(2,128)(2,1)} %channelize.1), calls=%async_computation | async-start | bytes 98304 | tf_op jit(solution)/shard_map/all_to_all | solution.py:419
  62.3 3.1 %collective-permute-start = (f32[2,2,4,24]{3,2,1,0:T(4,128)S(1)}, f32[2,2,4,24]{3,2,1,0:T(4,128)S(1)}, u32[]{:S(2)}, u32[]{:S(2)}) collective-permute-start(f32[2,2,4,24]{3,2,1,0:T(4,128)S(1)} %get-tuple-element.8), channel_id=1, source_target_pairs={{0,1},{1,0},{2,3},{3,2},{4,5},{5,4},{6,7},{7,6},{8,9},{9,8},{10,11... | collective-permute-start | bytes 4616 | tf_op jit(solution)/shard_map/ppermute | solution.py:437

commit v6 on v5

--- a/solution.py
+++ b/solution.py
@@ -125,7 +125,6 @@
 
 
 def adapt_kernel(
-    place_ref,
     code_ref,
     chunks_ref,
     steer_re_ref,
@@ -147,6 +146,8 @@
 ):
     chunk_count, _, _, elements = chunks_ref.shape
     _, bin_dev, beams, _ = own_ref.shape
+    position = lax.axis_index("rng")
+    core = position & (bin_dev - 1)
     gate_dev = (chunks_ref.shape[2] - MASK_ROWS) // 2
     gates = chunk_count * gate_dev
     f32, bf16 = jnp.float32, jnp.bfloat16
@@ -158,7 +159,7 @@
     )
     masks = []
     for c in range(chunk_count):
-        chunk = chunks_ref[c, place_ref[0]].astype(f32)
+        chunk = chunks_ref[c, core].astype(f32)
         at = HEAD + c * gate_dev
         sig_re[at : at + gate_dev] = chunk[:gate_dev]
         sig_im[at : at + gate_dev] = chunk[gate_dev : 2 * gate_dev]
@@ -173,8 +174,8 @@
     band_re = jnp.zeros((TILE, LANES), f32)
     band_im = jnp.zeros((TILE, LANES), f32)
     for t in range(2 * CODE_REACH + 1):
-        band_re = jnp.where(tap == t, code_ref[0, t], band_re)
-        band_im = jnp.where(tap == t, code_ref[1, t], band_im)
+        band_re = jnp.where(tap == t, code_ref[0:1, t : t + 1], band_re)
+        band_im = jnp.where(tap == t, code_ref[1:2, t : t + 1], band_im)
     band = jnp.concatenate(
         [
             jnp.concatenate([band_re, -band_im], axis=1),
@@ -212,8 +213,8 @@
     sides = []
     for steer_ref, ref in ((steer_re_ref, x_re), (steer_im_ref, x_im)):
         sides.append(steer_ref[...])
-        for slot in (1, 2):
-            at = pl.multiple_of(place_ref[slot] * gate_dev, 8)
+        for place in (position, position ^ 1):
+            at = pl.multiple_of(place * gate_dev, 8)
             sides.append(ref[pl.ds(at, gate_dev)])
         sides.append(spare)
     mat[:, 2 * elements :] = jnp.concatenate(sides, axis=0).T
@@ -269,8 +270,10 @@
                 ref[nxt:, seen : seen + 2 * BLOCK] = part
 
     whitened = mat[:, 2 * elements :]
-    inner = mm(whitened, whitened, TN)
-    top, low = inner[0:8], pltpu.roll(inner[64:72], 64, 1)
+    upright = whitened.T
+    beams_only = jnp.concatenate([upright[0:8], upright[64:72]], axis=0)
+    inner = dot6(split3(beams_only), split3(whitened))
+    top, low = inner[0:8], pltpu.roll(inner[8:16], 64, 1)
     real = top + low
     imag = pltpu.roll(top - low, 64, 1)
     own_lane = lax.broadcasted_iota(jnp.int32, (8, LANES), 1) == lax.broadcasted_iota(
@@ -284,42 +287,37 @@
         for part in range(2):
             rows = moved[8 * part : 8 * part + beams, :gate_dev]
             for b in range(bin_dev):
-                ref[part, b] = jnp.where(place_ref[0] == b, rows, 0.0)
-
-
-def adapt(place, code, chunks, steer_re, steer_im, beams):
+                ref[part, b] = jnp.where(core == b, rows, 0.0)
+
+
+def adapt(code, chunks, steer_re, steer_im, beams):
     count, bin_dev, rows, elements = chunks.shape
     gate_dev = (rows - MASK_ROWS) // 2
     gates = count * gate_dev
     width = 2 * elements + LANES
     out = (2, bin_dev, beams, gate_dev)
     f32, bf16 = jnp.float32, jnp.bfloat16
+    on_chip = [
+        pltpu.with_memory_space_constraint(x, pltpu.VMEM)
+        for x in (code, chunks, steer_re, steer_im)
+    ]
     return pl.pallas_call(
         adapt_kernel,
-        grid_spec=pltpu.PrefetchScalarGridSpec(
-            num_scalar_prefetch=1,
-            grid=(1,),
-            in_specs=[
-                pl.BlockSpec(memory_space=pltpu.SMEM),
-                pl.BlockSpec(memory_space=pltpu.VMEM),
-                pl.BlockSpec(memory_space=pltpu.VMEM),
-                pl.BlockSpec(memory_space=pltpu.VMEM),
-            ],
-            out_specs=[pl.BlockSpec(memory_space=pltpu.VMEM)] * 2,
-            scratch_shapes=[
-                pltpu.VMEM((gates - TILE + LANES + HEAD, elements), f32),
-                pltpu.VMEM((gates - TILE + LANES + HEAD, elements), f32),
-                pltpu.VMEM((gates, elements), f32),
-                pltpu.VMEM((gates, elements), f32),
-                pltpu.VMEM((gates, 2 * elements), bf16),
-                pltpu.VMEM((elements, width), f32),
-            ]
-            + [pltpu.VMEM((2 * elements, width), bf16)] * 3
-            + [pltpu.VMEM((elements, 2 * elements), bf16)] * 3,
-        ),
+        in_specs=[pl.BlockSpec(memory_space=pltpu.VMEM)] * 4,
+        out_specs=[pl.BlockSpec(memory_space=pltpu.VMEM)] * 2,
         out_shape=[pltpu.VMEM(out, f32)] * 2,
+        scratch_shapes=[
+            pltpu.VMEM((gates - TILE + LANES + HEAD, elements), f32),
+            pltpu.VMEM((gates - TILE + LANES + HEAD, elements), f32),
+            pltpu.VMEM((gates, elements), f32),
+            pltpu.VMEM((gates, elements), f32),
+            pltpu.VMEM((gates, 2 * elements), bf16),
+            pltpu.VMEM((elements, width), f32),
+        ]
+        + [pltpu.VMEM((2 * elements, width), bf16)] * 3
+        + [pltpu.VMEM((elements, 2 * elements), bf16)] * 3,
         name="adapt",
-    )(place, code, chunks, steer_re, steer_im)
+    )(*on_chip)
 
 
 def channel_kernel(
@@ -425,15 +423,10 @@
     )
     chunk = jnp.concatenate([turned, mask], axis=1)
     chunks = lax.all_gather(chunk, "rng", axis=0, tiled=False)
-    position = lax.axis_index("rng")
-    core = position % bin_dev
-    place = jnp.stack([core, position, position ^ 1]).astype(jnp.int32)
+    core = lax.axis_index("rng") % bin_dev
     steer_row = lax.dynamic_index_in_dim(steer_index, core, 0, keepdims=False)
     steer_re, steer_im = steering_rows(steer_row, elements)
-    chunks, steer_re, steer_im = (
-        pltpu.with_memory_space_constraint(x, pltpu.VMEM) for x in (chunks, steer_re, steer_im)
-    )
-    own, other = adapt(place, range_code, chunks, steer_re, steer_im, beams)
+    own, other = adapt(range_code, chunks, steer_re, steer_im, beams)
     swapped = lax.ppermute(other, "rng", [(i, i ^ 1) for i in range(rng_count)])
     return own + swapped
 

time: 66.2 us -> 64.8 us (0.979)
  Pallas kernels: 17.3 us -> 16 us
    pallas_call x1, Pallas kernels: 14.1 us -> 12.7 us  [adapt(): pl.pallas_call(adapt_kernel, in_specs=[pl.BlockSpec(memory_space=pltpu.VM...]
  transfers between devices with their start and end apart: 2 -> 2, of which waited for: 2 -> 2; matrix products, arithmetic and copies ran while one was open for 1% -> 0% of each run, Pallas kernels for 0% -> 0%
where the time goes in v6:
time: 64.8 us; the launch traced here: 64.6 us
  blocking collectives  22 us (34%)
  Pallas kernels  16 us (25%)
  starting transfers between devices  15.8 us (24%)
  waiting for transfers between devices  9.49 us (15%)
  other arithmetic  0.75 us (1%)
    all_gather x1, blocking collectives, shards(): chunks = lax.all_gather(chunk, 'rng', axis=0, tiled=False)  22 us
    all_to_all x1, starting transfers between devices, shards(): lax.all_to_all(spectra, 'dop', split_axis=0, concat_axis=0, tiled=True)  13.7 us
    pallas_call x1, Pallas kernels, adapt(): pl.pallas_call(adapt_kernel, in_specs=[pl.BlockSpec(memory_space=pltpu.VM...  12.7 us
    all_to_all x1, waiting for transfers between devices, shards(): lax.all_to_all(spectra, 'dop', split_axis=0, concat_axis=0, tiled=True)  8.51 us
    pallas_call x1, Pallas kernels, channelize(): pl.pallas_call(channel_kernel, in_specs=[pl.BlockSpec(memory_space=pl.ANY...  3.26 us
    ppermute x1, starting transfers between devices, shards(): swapped = lax.ppermute(other, 'rng', [(i, i ^ 1) for i in range(rng_count)])  2.07 us
  transfers between devices with their start and end apart: 2, of which 2 were waited for; matrix products, arithmetic and copies ran while one was open for 0% of the time, Pallas kernels for 0%

profile of v6, /device:TPU:1, one launch (start us, length us, event | category | flops | bytes accessed | tf_op | source)
XLA Modules:
  0.0 64.6 jit_solution(17022443967822823783)
XLA Ops:
  0.0 0.0 copy-start.1
  0.0 0.0 copy-start.2
  0.0 0.0 copy-start
  0.0 3.3 %channelize.1 = bf16[32,2,384]{2,1,0:T(2,128)(2,1)} custom-call(bf16[12288,128]{1,0:T(8,128)(2,1)} %bitcast.15, f32[8,512]{1,0:T(8,128)} %taps_hbm.1, bf16[128,512]{1,0:T(8,128)(2,1)} %constant.48.clone.table_hbm), custom_call_target="tpu_custom_call" | custom-call | tf_op jit(solution)/shard_map/channelize/pallas_call | solution.py:384
  3.3 13.7 %all-to-all-start = ((bf16[32,2,384]{2,1,0:T(2,128)(2,1)}), bf16[32,2,384]{2,1,0:T(2,128)(2,1)S(1)}, u32[]{:S(2)}, u32[]{:S(2)}) async-start(bf16[32,2,384]{2,1,0:T(2,128)(2,1)} %channelize.1), calls=%async_computation | async-start | bytes 98304 | tf_op jit(solution)/shard_map/all_to_all | solution.py:417
  17.0 0.0 copy-done.1
  17.0 0.1 fusion.5
  17.2 0.0 copy-done.2
  17.2 8.5 %all-to-all-done = bf16[32,2,384]{2,1,0:T(2,128)(2,1)S(1)} async-done(((bf16[32,2,384]{2,1,0:T(2,128)(2,1)}), bf16[32,2,384]{2,1,0:T(2,128)(2,1)S(1)}, u32[]{:S(2)}, u32[]{:S(2)}) %all-to-all-start) | async-done | bytes 49184 | tf_op jit(solution)/shard_map/all_to_all | solution.py:417
  25.7 0.2 copy.16
  25.9 0.2 copy.17
  26.1 0.1 copy.18
  26.2 22.0 %all-gather = bf16[32,56,256]{2,1,0:T(8,128)(2,1)S(1)} all-gather(bf16[2,56,256]{2,1,0:T(8,128)(2,1)S(1)} %fusion.1), channel_id=2, replica_groups=mesh['dop'=32,'rng'=16] {'rng'}, dimensions={0}, use_global_device_ids=true | all-gather | bytes 974848 | tf_op jit(solution)/shard_map/all_gather | solution.py:425
  48.2 0.0 copy-done
  48.2 12.7 %adapt.1 = (f32[2,2,4,24]{3,2,1,0:T(4,128)S(1)}, f32[2,2,4,24]{3,2,1,0:T(4,128)S(1)}) custom-call(f32[2,7]{1,0:T(2,128)S(1)} %copy-done, bf16[16,2,56,256]{3,2,1,0:T(8,128)(2,1)S(1)} %bitcast.14, f32[8,256]{1,0:T(8,128)S(1)} %pad.12.steer_re_ref, f32[8,256]{1,0:T(8,128)S(1)} %pad.13.steer_im_ref), custom_call_target="tpu_custom_call" | custom-call | tf_op jit(solution)/shard_map/adapt/pallas_call | solution.py:304
  61.0 2.1 %collective-permute-start = (f32[2,2,4,24]{3,2,1,0:T(4,128)S(1)}, f32[2,2,4,24]{3,2,1,0:T(4,128)S(1)}, u32[]{:S(2)}, u32[]{:S(2)}) collective-permute-start(f32[2,2,4,24]{3,2,1,0:T(4,128)S(1)} %get-tuple-element.8), channel_id=1, source_target_pairs={{0,1},{1,0},{2,3},{3,2},{4,5},{5,4},{6,7},{7,6},{8,9},{9,8},{10,11... | collective-permute-start | bytes 4616 | tf_op jit(solution)/shard_map/ppermute | solution.py:430
  63.1 1.0 %collective-permute-done = f32[2,2,4,24]{3,2,1,0:T(4,128)S(1)} collective-permute-done((f32[2,2,4,24]{3,2,1,0:T(4,128)S(1)}, f32[2,2,4,24]{3,2,1,0:T(4,128)S(1)}, u32[]{:S(2)}, u32[]{:S(2)}) %collective-permute-start) | collective-permute-done | bytes 1568 | tf_op jit(solution)/shard_map/ppermute | solution.py:430
  64.0 0.6 add.33
  (6 shorter events, 0.0 us)
Async XLA Ops:
  0.0 17.0 %copy-start.1 = (s32[2,4]{1,0:T(2,128)S(1)}, s32[2,4]{1,0:T(2,128)}, u32[]{:S(2)}) copy-start(s32[2,4]{1,0:T(2,128)} %param.10) | copy-start | bytes 100
  0.0 17.2 %copy-start.2 = (s32[2,24]{1,0:T(2,128)S(1)}, s32[2,24]{1,0:T(2,128)}, u32[]{:S(2)}) copy-start(s32[2,24]{1,0:T(2,128)} %param.9) | copy-start | bytes 580
  0.0 48.2 %copy-start = (f32[2,7]{1,0:T(2,128)S(1)}, f32[2,7]{1,0:T(2,128)}, u32[]{:S(2)}) copy-start(f32[2,7]{1,0:T(2,128)} %code_ref.1) | copy-start | bytes 172
  3.3 22.5 %all-to-all-start = ((bf16[32,2,384]{2,1,0:T(2,128)(2,1)}), bf16[32,2,384]{2,1,0:T(2,128)(2,1)S(1)}, u32[]{:S(2)}, u32[]{:S(2)}) async-start(bf16[32,2,384]{2,1,0:T(2,128)(2,1)} %channelize.1), calls=%async_computation | async-start | bytes 98304 | tf_op jit(solution)/shard_map/all_to_all | solution.py:417
  61.0 3.1 %collective-permute-start = (f32[2,2,4,24]{3,2,1,0:T(4,128)S(1)}, f32[2,2,4,24]{3,2,1,0:T(4,128)S(1)}, u32[]{:S(2)}, u32[]{:S(2)}) collective-permute-start(f32[2,2,4,24]{3,2,1,0:T(4,128)S(1)} %get-tuple-element.8), channel_id=1, source_target_pairs={{0,1},{1,0},{2,3},{3,2},{4,5},{5,4},{6,7},{7,6},{8,9},{9,8},{10,11... | collective-permute-start | bytes 4616 | tf_op jit(solution)/shard_map/ppermute | solution.py:430

commit v7 on v6

--- a/solution.py
+++ b/solution.py
@@ -144,11 +144,11 @@
     s_mid,
     s_low,
 ):
-    chunk_count, _, _, elements = chunks_ref.shape
-    _, bin_dev, beams, _ = own_ref.shape
+    chunk_count, tiles, _, elements = chunks_ref.shape
+    _, bin_dev, beams, gate_dev = own_ref.shape
+    per_bin = (tiles - 1) // bin_dev
     position = lax.axis_index("rng")
     core = position & (bin_dev - 1)
-    gate_dev = (chunks_ref.shape[2] - MASK_ROWS) // 2
     gates = chunk_count * gate_dev
     f32, bf16 = jnp.float32, jnp.bfloat16
     for ref in (sig_re, sig_im):
@@ -159,11 +159,13 @@
     )
     masks = []
     for c in range(chunk_count):
-        chunk = chunks_ref[c, core].astype(f32)
+        chunk = chunks_ref[c, pl.ds(core * per_bin, per_bin)].astype(f32)
+        chunk = chunk.reshape(2 * gate_dev, elements)
         at = HEAD + c * gate_dev
         sig_re[at : at + gate_dev] = chunk[:gate_dev]
         sig_im[at : at + gate_dev] = chunk[gate_dev : 2 * gate_dev]
-        mask_row = chunk[2 * gate_dev : 2 * gate_dev + 1, :LANES]
+        rows = chunks_ref[c, tiles - 1, :, :LANES].astype(f32)
+        mask_row = jnp.where(core == 0, rows[0:1], rows[1:2])
         masks.append(jnp.sum(jnp.where(diagonal, mask_row, 0.0), axis=1, keepdims=True))
 
     tap = (
@@ -290,9 +292,9 @@
                 ref[part, b] = jnp.where(core == b, rows, 0.0)
 
 
-def adapt(code, chunks, steer_re, steer_im, beams):
-    count, bin_dev, rows, elements = chunks.shape
-    gate_dev = (rows - MASK_ROWS) // 2
+def adapt(code, chunks, steer_re, steer_im, bin_dev, beams):
+    count, tiles, _, elements = chunks.shape
+    gate_dev = (tiles - 1) * MASK_ROWS // (2 * bin_dev)
     gates = count * gate_dev
     width = 2 * elements + LANES
     out = (2, bin_dev, beams, gate_dev)
@@ -418,15 +420,15 @@
     turned = turned.reshape(dop_count, bin_dev, 2 * gate_dev, elem_dev)
     turned = jnp.transpose(turned, (1, 2, 0, 3)).reshape(bin_dev, 2 * gate_dev, elements)
     mask = jnp.pad(
-        train_mask.astype(jnp.bfloat16)[:, None, :],
-        ((0, 0), (0, MASK_ROWS - 1), (0, elements - gate_dev)),
-    )
-    chunk = jnp.concatenate([turned, mask], axis=1)
+        train_mask.astype(jnp.bfloat16), ((0, MASK_ROWS - bin_dev), (0, elements - gate_dev))
+    )
+    turned = turned.reshape(-1, MASK_ROWS, elements)
+    chunk = jnp.concatenate([turned, mask[None]], axis=0)
     chunks = lax.all_gather(chunk, "rng", axis=0, tiled=False)
     core = lax.axis_index("rng") % bin_dev
     steer_row = lax.dynamic_index_in_dim(steer_index, core, 0, keepdims=False)
     steer_re, steer_im = steering_rows(steer_row, elements)
-    own, other = adapt(range_code, chunks, steer_re, steer_im, beams)
+    own, other = adapt(range_code, chunks, steer_re, steer_im, bin_dev, beams)
     swapped = lax.ppermute(other, "rng", [(i, i ^ 1) for i in range(rng_count)])
     return own + swapped
 

time: 64.8 us -> 65.8 us (1.015)
  local copies, waits for them, and re-layouts: 0.5 us -> 1.61 us
    another operation x0 -> x1, local copies, waits for them, and re-layouts: none -> 1.02 us  [shards(): turned = turned.reshape(-1, MASK_ROWS, elements)]
where the time goes in v7:
time: 65.8 us; the launch traced here: 65.6 us
  blocking collectives  21.8 us (33%)
  Pallas kernels  16 us (24%)
  starting transfers between devices  15.8 us (24%)
  waiting for transfers between devices  9.49 us (14%)
  local copies, waits for them, and re-layouts  1.61 us (2%)
  other arithmetic  0.75 us (1%)
    all_gather x1, blocking collectives, shards(): chunks = lax.all_gather(chunk, 'rng', axis=0, tiled=False)  21.8 us
    all_to_all x1, starting transfers between devices, shards(): lax.all_to_all(spectra, 'dop', split_axis=0, concat_axis=0, tiled=True)  13.7 us
    pallas_call x1, Pallas kernels, adapt(): pl.pallas_call(adapt_kernel, in_specs=[pl.BlockSpec(memory_space=pltpu.VM...  12.8 us
    all_to_all x1, waiting for transfers between devices, shards(): lax.all_to_all(spectra, 'dop', split_axis=0, concat_axis=0, tiled=True)  8.5 us
    pallas_call x1, Pallas kernels, channelize(): pl.pallas_call(channel_kernel, in_specs=[pl.BlockSpec(memory_space=pl.ANY...  3.26 us
    ppermute x1, starting transfers between devices, shards(): swapped = lax.ppermute(other, 'rng', [(i, i ^ 1) for i in range(rng_count)])  2.06 us
  transfers between devices with their start and end apart: 2, of which 2 were waited for; matrix products, arithmetic and copies ran while one was open for 0% of the time, Pallas kernels for 0%

profile of v7, /device:TPU:1, one launch (start us, length us, event | category | flops | bytes accessed | tf_op | source)
XLA Modules:
  0.0 65.6 jit_solution(15666585956628583026)
XLA Ops:
  0.0 0.0 copy-start.1
  0.0 0.0 copy-start.2
  0.0 0.0 copy-start
  0.0 3.3 %channelize.1 = bf16[32,2,384]{2,1,0:T(2,128)(2,1)} custom-call(bf16[12288,128]{1,0:T(8,128)(2,1)} %bitcast.16, f32[8,512]{1,0:T(8,128)} %taps_hbm.1, bf16[128,512]{1,0:T(8,128)(2,1)} %constant.48.clone.table_hbm), custom_call_target="tpu_custom_call" | custom-call | tf_op jit(solution)/shard_map/channelize/pallas_call | solution.py:386
  3.3 13.7 %all-to-all-start = ((bf16[32,2,384]{2,1,0:T(2,128)(2,1)}), bf16[32,2,384]{2,1,0:T(2,128)(2,1)S(1)}, u32[]{:S(2)}, u32[]{:S(2)}) async-start(bf16[32,2,384]{2,1,0:T(2,128)(2,1)} %channelize.1), calls=%async_computation | async-start | bytes 98304 | tf_op jit(solution)/shard_map/all_to_all | solution.py:419
  17.0 0.0 copy-done.1
  17.0 0.0 copy-done.2
  17.1 0.1 fusion.3
  17.2 8.5 %all-to-all-done = bf16[32,2,384]{2,1,0:T(2,128)(2,1)S(1)} async-done(((bf16[32,2,384]{2,1,0:T(2,128)(2,1)}), bf16[32,2,384]{2,1,0:T(2,128)(2,1)S(1)}, u32[]{:S(2)}, u32[]{:S(2)}) %all-to-all-start) | async-done | bytes 49184 | tf_op jit(solution)/shard_map/all_to_all | solution.py:419
  25.7 0.2 copy.13
  25.9 0.4 copy.14
  26.3 1.0 %reshape_reshape.3 = bf16[12,8,256]{2,1,0:T(8,128)(2,1)S(1)} reshape(bf16[2,48,32,8]{3,2,1,0:T(8,128)(2,1)S(1)} %copy.14) | data formatting | bytes 98304 | tf_op jit(solution)/shard_map/reshape;reshape | solution.py:425
  27.3 21.8 %all-gather = bf16[208,8,256]{2,1,0:T(8,128)(2,1)S(1)} all-gather(bf16[13,8,256]{2,1,0:T(8,128)(2,1)S(1)} %pad_maximum_fusion), channel_id=2, replica_groups=mesh['dop'=32,'rng'=16] {'rng'}, dimensions={0}, use_global_device_ids=true | all-gather | bytes 905216 | tf_op jit(solution)/shard_map/all_gather | solution.py:427
  49.2 0.0 copy-done
  49.2 12.8 %adapt.1 = (f32[2,2,4,24]{3,2,1,0:T(4,128)S(1)}, f32[2,2,4,24]{3,2,1,0:T(4,128)S(1)}) custom-call(f32[2,7]{1,0:T(2,128)S(1)} %copy-done, bf16[16,13,8,256]{3,2,1,0:T(8,128)(2,1)S(1)} %bitcast.15, f32[8,256]{1,0:T(8,128)S(1)} %pad.12.steer_re_ref, f32[8,256]{1,0:T(8,128)S(1)} %pad.13.steer_im_ref), custom_call_target="tpu_custom_call" | custom-call | tf_op jit(solution)/shard_map/adapt/pallas_call | solution.py:306
  61.9 2.1 %collective-permute-start = (f32[2,2,4,24]{3,2,1,0:T(4,128)S(1)}, f32[2,2,4,24]{3,2,1,0:T(4,128)S(1)}, u32[]{:S(2)}, u32[]{:S(2)}) collective-permute-start(f32[2,2,4,24]{3,2,1,0:T(4,128)S(1)} %get-tuple-element.8), channel_id=1, source_target_pairs={{0,1},{1,0},{2,3},{3,2},{4,5},{5,4},{6,7},{7,6},{8,9},{9,8},{10,11... | collective-permute-start | bytes 4616 | tf_op jit(solution)/shard_map/ppermute | solution.py:432
  64.0 1.0 %collective-permute-done = f32[2,2,4,24]{3,2,1,0:T(4,128)S(1)} collective-permute-done((f32[2,2,4,24]{3,2,1,0:T(4,128)S(1)}, f32[2,2,4,24]{3,2,1,0:T(4,128)S(1)}, u32[]{:S(2)}, u32[]{:S(2)}) %collective-permute-start) | collective-permute-done | bytes 1568 | tf_op jit(solution)/shard_map/ppermute | solution.py:432
  65.0 0.6 add.33
  (6 shorter events, 0.0 us)
Async XLA Ops:
  0.0 17.0 %copy-start.1 = (s32[2,24]{1,0:T(2,128)S(1)}, s32[2,24]{1,0:T(2,128)}, u32[]{:S(2)}) copy-start(s32[2,24]{1,0:T(2,128)} %param.9) | copy-start | bytes 580
  0.0 17.0 %copy-start.2 = (s32[2,4]{1,0:T(2,128)S(1)}, s32[2,4]{1,0:T(2,128)}, u32[]{:S(2)}) copy-start(s32[2,4]{1,0:T(2,128)} %param.10) | copy-start | bytes 100
  0.0 49.2 %copy-start = (f32[2,7]{1,0:T(2,128)S(1)}, f32[2,7]{1,0:T(2,128)}, u32[]{:S(2)}) copy-start(f32[2,7]{1,0:T(2,128)} %code_ref.1) | copy-start | bytes 172
  3.3 22.5 %all-to-all-start = ((bf16[32,2,384]{2,1,0:T(2,128)(2,1)}), bf16[32,2,384]{2,1,0:T(2,128)(2,1)S(1)}, u32[]{:S(2)}, u32[]{:S(2)}) async-start(bf16[32,2,384]{2,1,0:T(2,128)(2,1)} %channelize.1), calls=%async_computation | async-start | bytes 98304 | tf_op jit(solution)/shard_map/all_to_all | solution.py:419
  61.9 3.1 %collective-permute-start = (f32[2,2,4,24]{3,2,1,0:T(4,128)S(1)}, f32[2,2,4,24]{3,2,1,0:T(4,128)S(1)}, u32[]{:S(2)}, u32[]{:S(2)}) collective-permute-start(f32[2,2,4,24]{3,2,1,0:T(4,128)S(1)} %get-tuple-element.8), channel_id=1, source_target_pairs={{0,1},{1,0},{2,3},{3,2},{4,5},{5,4},{6,7},{7,6},{8,9},{9,8},{10,11... | collective-permute-start | bytes 4616 | tf_op jit(solution)/shard_map/ppermute | solution.py:432
